TPU v7x, 32 devices: a whole 2x2x4 slice. The times are simulated.
32 devices in a mesh: groups: 2 (over x), tm: 8 (over z, y), rows: 2 (over core).
Axes of the slice: x: 2, y: 2, z: 4, core: 2. Of those that a mesh axis runs over, the one named last changes fastest.
Arguments:
- frames_in: bfloat16 [4, 8, 16, 256, 128], P('groups', 'tm', 'rows'), parts along dimension 0, may hold values from -12 to 12
- gain_one: float32 [128], replicated, may hold values from 0.25 to 1.75
- norm_bias_one: float32 [128], replicated, may hold values from -3 to 3
- kernel_one: bfloat16 [3, 3, 3, 128, 128], replicated, may hold values from -0.109375 to 0.109375
- bias_one: float32 [128], replicated, may hold values from -2 to 2
- gain_two: float32 [128], replicated, may hold values from 0.25 to 1.75
- norm_bias_two: float32 [128], replicated, may hold values from -3 to 3
- kernel_two: bfloat16 [3, 3, 3, 128, 128], replicated, may hold values from -0.109375 to 0.109375
- bias_two: float32 [128], replicated, may hold values from -2 to 2
- kernel_down: bfloat16 [3, 3, 128, 128], replicated, may hold values from -0.1875 to 0.1875
- bias_down: float32 [128], replicated, may hold values from -2 to 2
Outputs:
- features_down: bfloat16 [4, 8, 8, 128, 128], P('groups', 'tm', 'rows'), parts along dimension 0
There are 2 independent parts, one for each index of `groups`. A program takes and returns all parts, laid end to end along the dimension named above; an argument that names none is the same for every part. Nothing has to cross between parts.
All inputs are finite; a program needn't handle non-finite values.
Results may differ from a plain program's by a relative error of at most 0.0095.
Values may be sent and summed in bfloat16 or wider, within the bound.
No kernel may reach another device: no remote copies, remote signals or barrier semaphores. Data moves between devices by JAX's collectives and lax.ppermute only.
A program may use at most 128 MiB of HBM per device.

v0:
```python
import functools

import jax
import jax.numpy as jnp
from jax import lax
from jax.experimental import pallas as pl
from jax.experimental.pallas import tpu as pltpu
from jax.sharding import PartitionSpec as P


G = 32
EPSILON = 1e-06
F32 = jnp.float32
BF16 = jnp.bfloat16


def norm_params(totals, gain, bias, cells):
    channels = totals.shape[1]
    size = channels // G
    left = lax.broadcasted_iota(jnp.int32, (channels, channels), 0) // size
    right = lax.broadcasted_iota(jnp.int32, (channels, channels), 1) // size
    same = (left == right).astype(F32)
    grouped = jnp.dot(totals, same, precision=lax.Precision.HIGHEST, preferred_element_type=F32)
    grouped = grouped / (cells * size)
    mean = grouped[0:1]
    inverse = lax.rsqrt(grouped[1:2] - mean * mean + EPSILON)
    return mean, inverse * gain, bias


def fill_row(stack, r, values, params):
    mean, scale, bias = params
    width, channels = values.shape
    half = 0.5 * ((values.astype(F32) - mean) * scale + bias)
    normed = half + half * jnp.tanh(half)
    column = lax.broadcasted_iota(jnp.int32, (width, channels), 0)
    before = jnp.where(column == 0, 0.0, pltpu.roll(normed, 1, 0))
    after = jnp.where(column == width - 1, 0.0, pltpu.roll(normed, width - 1, 0))
    stack[r, :, 0:channels] = before.astype(BF16)
    stack[r, :, channels : 2 * channels] = normed.astype(BF16)
    stack[r, :, 2 * channels :] = after.astype(BF16)


def fill_frame(stack, values, params):
    for r, value in enumerate(values):
        fill_row(stack, r, value(), params)


def close_stack(stack):
    last = stack.shape[0] - 1
    stack[last] = jnp.zeros(stack.shape[1:], BF16)


def taps(stack, weights, start, count):
    rows = [
        jnp.concatenate([stack[r], stack[r + 1], stack[r + 2]], axis=1)
        for r in range(start, start + count)
    ]
    return jnp.dot(jnp.concatenate(rows, axis=0), weights, preferred_element_type=F32)


def steps(first, last):
    total = last - first
    size = 3 if total % 3 == 0 else 2
    return [(r, min(size, last - r)) for r in range(first, last, size)]


def reader(ref, r):
    return lambda: ref[r]


def choose(flags, r, part, k, own, mate):
    def read():
        return jnp.where(flags[1] == 1, jnp.where(flags[0] == 0, own[r], mate[r]), part[k])

    return read


def place_kernel(flags, x_ref, own_ref, other_ref):
    height = x_ref.shape[1]
    side, band = flags[0], flags[2]
    for r in range(height):
        row = jnp.where(band == 0, height - 1 - r, r)
        own_ref[r] = x_ref[side, row]
        other_ref[r] = x_ref[1 - side, row]


def sums_kernel(x_ref, out_ref):
    clips, height, width, channels = x_ref.shape
    for c in range(clips):
        total = jnp.zeros((8, channels), F32)
        square = jnp.zeros((8, channels), F32)
        for r in range(height):
            v = x_ref[c, r].astype(F32).reshape(width // 8, 8, channels)
            total += jnp.sum(v, axis=0)
            square += jnp.sum(v * v, axis=0)
        out_ref[c, 0:1] = jnp.sum(total, axis=0, keepdims=True)
        out_ref[c, 1:2] = jnp.sum(square, axis=0, keepdims=True)
        out_ref[c, 2:8] = jnp.zeros((6, channels), F32)


def own_kernel(cells, flags, x_ref, e_ref, t_ref, g_ref, c_ref, w_ref, acc_ref, stack):
    height, width, _ = x_ref.shape
    params = norm_params(t_ref[...], g_ref[...], c_ref[...], cells)
    fill_frame(stack, [reader(e_ref, 0)] + [reader(x_ref, r) for r in range(height)], params)
    close_stack(stack)
    for start, count in steps(0, height):
        part = taps(stack, w_ref[...], start, count)
        acc_ref[start : start + count] = part.reshape(count, width, -1)


def mates_kernel(cells, flags, m_ref, em_ref, tm_ref, p_ref, ep_ref, tp_ref, o_ref, eo_ref, to_ref, g_ref, c_ref, wm_ref, wp_ref, in_ref, acc_ref, xm, xp):
    height, width, _ = m_ref.shape
    first, even = flags[1] == 1, flags[0] == 0
    params = norm_params(tm_ref[...], g_ref[...], c_ref[...], cells)
    fill_frame(xm, [reader(em_ref, 0)] + [reader(m_ref, r) for r in range(height)], params)
    close_stack(xm)
    totals = jnp.where(first, jnp.where(even, to_ref[...], tm_ref[...]), tp_ref[...])
    params = norm_params(totals, g_ref[...], c_ref[...], cells)
    values = [choose(flags, 0, ep_ref, 0, eo_ref, em_ref)]
    values += [choose(flags, r, p_ref, r, o_ref, m_ref) for r in range(height)]
    fill_frame(xp, values, params)
    close_stack(xp)
    for start, count in steps(0, height):
        part = taps(xm, wm_ref[...], start, count) + taps(xp, wp_ref[...], start, count)
        acc_ref[start : start + count] = in_ref[start : start + count] + part.reshape(count, width, -1)


def hidden_rows(stack, w_ref, in_ref, bias_ref, first, a_ref, b_ref, sum_ref):
    rows, width, channels = a_ref.shape
    both = 2 * channels
    total = jnp.zeros((8, both), F32)
    square = jnp.zeros((8, both), F32)
    for start, count in steps(0, rows):
        part = taps(stack, w_ref[...], start, count).reshape(count, width, both)
        begin = first + start
        hidden = (in_ref[begin : begin + count] + part + bias_ref[...]).astype(BF16)
        a_ref[start : start + count] = hidden[:, :, :channels]
        b_ref[start : start + count] = hidden[:, :, channels:]
        wide = hidden.astype(F32).reshape(count * width // 8, 8, both)
        total += jnp.sum(wide, axis=0)
        square += jnp.sum(wide * wide, axis=0)
    total = jnp.sum(total, axis=0, keepdims=True)
    square = jnp.sum(square, axis=0, keepdims=True)
    for k in range(2):
        sum_ref[k, 0:1] = total[:, k * channels : (k + 1) * channels]
        sum_ref[k, 1:2] = square[:, k * channels : (k + 1) * channels]
        sum_ref[k, 2:8] = jnp.zeros((6, channels), F32)


def near_kernel(cells, flags, p_ref, ep_ref, tp_ref, o_ref, eo_ref, to_ref, m_ref, em_ref, tm_ref, g_ref, c_ref, w_ref, in_ref, bias_ref, a_ref, b_ref, edge_ref, sum_ref, stack):
    totals = jnp.where(flags[1] == 1, jnp.where(flags[0] == 0, to_ref[...], tm_ref[...]), tp_ref[...])
    params = norm_params(totals, g_ref[...], c_ref[...], cells)
    values = [choose(flags, 0, ep_ref, 0, eo_ref, em_ref)]
    values += [choose(flags, r, p_ref, r, o_ref, m_ref) for r in range(p_ref.shape[0])]
    fill_frame(stack, values, params)
    hidden_rows(stack, w_ref, in_ref, bias_ref, 0, a_ref, b_ref, sum_ref)
    edge_ref[0] = a_ref[0:2]
    edge_ref[1] = b_ref[0:2]


def far_kernel(cells, flags, p_ref, q_ref, tp_ref, o_ref, to_ref, m_ref, tm_ref, g_ref, c_ref, w_ref, in_ref, bias_ref, a_ref, b_ref, sum_ref, stack):
    totals = jnp.where(flags[1] == 1, jnp.where(flags[0] == 0, to_ref[...], tm_ref[...]), tp_ref[...])
    params = norm_params(totals, g_ref[...], c_ref[...], cells)
    height, near = o_ref.shape[0], p_ref.shape[0]
    rows = a_ref.shape[0]
    values = []
    for r in range(height - rows - 1, height):
        part, k = (p_ref, r) if r < near else (q_ref, r - near)
        values.append(choose(flags, r, part, k, o_ref, m_ref))
    fill_frame(stack, values, params)
    close_stack(stack)
    hidden_rows(stack, w_ref, in_ref, bias_ref, height - rows, a_ref, b_ref, sum_ref)


def halves(edge, k, near, far):
    rows = [lambda: edge[k, 1], lambda: edge[k, 0]]
    rows += [reader(near, r) for r in range(near.shape[0])]
    return rows + [reader(far, r) for r in range(far.shape[0])]


def local_kernel(cells, flags, a1, a2, b1, b2, e_ref, t_ref, g_ref, c_ref, wa_ref, wb_ref, acc_ref, xa, xb):
    out_rows, width, _ = acc_ref.shape
    for k, (stack, near, far) in enumerate(((xa, a1, a2), (xb, b1, b2))):
        params = norm_params(t_ref[k], g_ref[...], c_ref[...], cells)
        fill_frame(stack, halves(e_ref, k, near, far), params)
        close_stack(stack)
    for start, count in steps(0, out_rows):
        part = taps(xa, wa_ref[...], start, count) + taps(xb, wb_ref[...], start, count)
        acc_ref[start : start + count] = part.reshape(count, width, -1)


def either(flags, first, other):
    return lambda: jnp.where(flags[1] == 1, first(), other())


def residual_row(raw, branch):
    return (raw.astype(F32) + branch).astype(BF16)


def put_row(res, r, value):
    res[r, 0 : value.shape[0], :] = value.astype(F32)


def down_rows(flags, res, wd_ref, bd_ref, height):
    half = (res.shape[1] - 8) // 2
    band = flags[2]
    rows = []
    for i in range(height // 2):
        cols = [
            res[2 * i + a + band, pl.ds(b, half, stride=2), :].astype(BF16)
            for a in range(3)
            for b in range(3)
        ]
        rows.append(jnp.concatenate(cols, axis=1))
    out = jnp.dot(jnp.concatenate(rows, axis=0), wd_ref[...], preferred_element_type=F32)
    out = (out + bd_ref[...]).astype(BF16)
    return out.reshape(height // 2, half, -1)


def out_row(flags, i, rows):
    return jnp.where(flags[2] == 0, rows - 1 - i, i)


def second_kernel(cells, flags, b1, b2, eb_ref, tp_ref, a1, a2, e_ref, t_ref, g_ref, c_ref, w_ref, in_ref, bias_ref, own, mate, eo_ref, em_ref, wd_ref, bd_ref, acc_ref, out_ref, stack, res):
    out_rows, width, channels = acc_ref.shape
    height = out_rows - 1
    even = flags[0] == 0
    params = norm_params(jnp.where(flags[1] == 1, t_ref[0], tp_ref[1]), g_ref[...], c_ref[...], cells)
    values = [
        either(flags, f, o) for f, o in zip(halves(e_ref, 0, a1, a2), halves(eb_ref, 0, b1, b2))
    ]
    fill_frame(stack, values, params)
    close_stack(stack)
    res[:, width:, :] = jnp.zeros((res.shape[0], res.shape[1] - width, channels), F32)
    res[out_rows] = jnp.zeros(res.shape[1:], F32)
    for start, count in steps(0, out_rows):
        part = taps(stack, w_ref[...], start, count).reshape(count, width, 2 * channels)
        branch = in_ref[start : start + count] + part + bias_ref[...]
        acc_ref[start : start + count] = branch[:, :, :channels]
        for k in range(count):
            r = start + k - 1
            raw = jnp.where(even, mate[r], own[r]) if r >= 0 else jnp.where(even, em_ref[0], eo_ref[0])
            put_row(res, r + 1, residual_row(raw, branch[k, :, channels:]))
    out = down_rows(flags, res, wd_ref, bd_ref, height)
    for i in range(height // 2):
        out_ref[out_row(flags, i, height // 2)] = out[i]


def first_near_kernel(cells, flags, p1, ep_ref, tp_ref, a1, e_ref, t_ref, g_ref, c_ref, w_ref, in_ref, own, mate, eo_ref, em_ref, out_ref, stack):
    rows, width, channels = out_ref.shape
    even = flags[0] == 0
    params = norm_params(jnp.where(flags[1] == 1, t_ref[0], tp_ref[0]), g_ref[...], c_ref[...], cells)
    firsts = [lambda: e_ref[0, 1], lambda: e_ref[0, 0]] + [reader(a1, r) for r in range(rows)]
    others = [lambda: ep_ref[0, 1], lambda: ep_ref[0, 0]] + [reader(p1, r) for r in range(rows)]
    fill_frame(stack, [either(flags, f, o) for f, o in zip(firsts, others)], params)
    for start, count in steps(0, rows):
        part = taps(stack, w_ref[...], start, count).reshape(count, width, channels)
        branch = in_ref[start : start + count] + part
        for k in range(count):
            r = start + k - 1
            raw = jnp.where(even, own[r], mate[r]) if r >= 0 else jnp.where(even, eo_ref[0], em_ref[0])
            out_ref[r + 1] = residual_row(raw, branch[k])


def first_far_kernel(cells, flags, p1, p2, tp_ref, a1, a2, t_ref, g_ref, c_ref, w_ref, in_ref, near_ref, other_ref, own, mate, wd_ref, bd_ref, send_ref, keep_ref, stack, res):
    out_rows, width, channels = in_ref.shape
    height = out_rows - 1
    half = p1.shape[0]
    done = near_ref.shape[0]
    even = flags[0] == 0
    params = norm_params(jnp.where(flags[1] == 1, t_ref[0], tp_ref[0]), g_ref[...], c_ref[...], cells)
    values = []
    for r in range(done - 2, height):
        f, o, k = (a1, p1, r) if r < half else (a2, p2, r - half)
        values.append(either(flags, reader(f, k), reader(o, k)))
    fill_frame(stack, values, params)
    close_stack(stack)
    res[:, width:, :] = jnp.zeros((res.shape[0], res.shape[1] - width, channels), F32)
    res[out_rows] = jnp.zeros(res.shape[1:], F32)
    for r in range(done):
        put_row(res, r, near_ref[r])
    for start, count in steps(0, out_rows - done):
        part = taps(stack, w_ref[...], start, count).reshape(count, width, channels)
        branch = in_ref[done + start : done + start + count] + part
        for k in range(count):
            r = done + start + k - 1
            put_row(res, r + 1, residual_row(jnp.where(even, own[r], mate[r]), branch[k]))
    out = down_rows(flags, res, wd_ref, bd_ref, height)
    for i in range(height // 2):
        row = out_row(flags, i, height // 2)
        other = other_ref[row]
        send_ref[row] = jnp.where(even, other, out[i])
        keep_ref[row] = jnp.where(even, out[i], other)


def call(kernel, out_shape, scratch, flags, *args, aliases=None, flops=0):
    vmem = pl.BlockSpec(memory_space=pltpu.VMEM)
    several = isinstance(out_shape, (list, tuple))
    moved = sum(a.size * a.dtype.itemsize for a in args)
    return pl.pallas_call(
        kernel,
        out_shape=out_shape,
        in_specs=[pl.BlockSpec(memory_space=pltpu.SMEM)] + [vmem] * len(args),
        out_specs=[vmem] * len(out_shape) if several else vmem,
        scratch_shapes=scratch,
        input_output_aliases=aliases or {},
        cost_estimate=pl.CostEstimate(flops=flops, bytes_accessed=moved, transcendentals=0),
        compiler_params=pltpu.CompilerParams(vmem_limit_bytes=32 << 20),
    )(flags, *args)


def slot_weights(kernel, band):
    channels = kernel.shape[-1]
    kernel = jnp.where(band == 0, kernel[::-1], kernel)
    by_frame = jnp.transpose(kernel, (2, 0, 1, 3, 4)).reshape(3, -1, channels)
    padded = jnp.pad(by_frame, ((1, 1), (0, 0), (0, 0)))
    return jnp.concatenate([padded[1:], padded[:-1]], axis=-1)


def local(
    frames_in,
    gain_one,
    norm_bias_one,
    kernel_one,
    bias_one,
    gain_two,
    norm_bias_two,
    kernel_two,
    bias_two,
    kernel_down,
    bias_down,
):
    x = frames_in[:, 0]
    clips, height, width, channels = x.shape
    count = lax.axis_size("tm")
    bands = lax.axis_size("rows")
    assert clips == 2 and bands == 2 and count % 2 == 0 and height % 4 == 0
    cells = height * bands * width
    near = height // 2
    position = lax.axis_index("tm")
    band = lax.axis_index("rows")
    side = position % 2
    even = side == 0
    flags = jnp.stack([side, (position < 2).astype(jnp.int32), band]).astype(jnp.int32)
    swap = [(i, i ^ 1) for i in range(count)]
    onward = [(i, (i + 2) % count) for i in range(count)]
    across = [(0, 1), (1, 0)]

    def swapped(v):
        return lax.ppermute(v, "tm", swap)

    def later(v):
        return lax.ppermute(v, "tm", onward)

    def beside(v):
        return lax.ppermute(v, "rows", across)

    def pick(pair, index):
        return lax.dynamic_index_in_dim(pair, index, 0, keepdims=False)

    def row(v):
        return v.reshape(1, -1)

    def stack(rows):
        return pltpu.VMEM((rows, width, 3 * channels), BF16)

    def flops(rows, slots):
        return 2 * rows * width * 9 * channels * 2 * channels * slots

    def shape(*dims, dtype=BF16):
        return jax.ShapeDtypeStruct(dims, dtype)

    def kernel(body, *rest, **options):
        return call(functools.partial(body, cells), *rest, **options)

    frame = (height, width, channels)
    own, other = call(place_kernel, [shape(*frame), shape(*frame)], [], flags, x)
    own_before = later(own)
    mate = swapped(other)
    partial = call_sums(x)
    totals = partial + beside(partial)
    own_total = pick(totals, side)
    mate_total = swapped(pick(totals, 1 - side))
    both_before = later(jnp.stack([own_total, mate_total]))
    own_edge = beside(own[:1])

    weights = slot_weights(kernel_one, band)
    norm_one = (row(gain_one), row(norm_bias_one))
    acc = kernel(
        own_kernel,
        shape(height, width, 2 * channels, dtype=F32),
        [stack(height + 2)],
        flags,
        own,
        own_edge,
        own_total,
        *norm_one,
        pick(weights, 2 + side),
        flops=flops(height, 1),
    )

    before_near = later(mate[: near + 1])
    before_far = later(mate[near + 1 :])
    mate_edge = beside(mate[:1])
    own_before_edge = beside(own_before[:1])
    acc = kernel(
        mates_kernel,
        shape(height, width, 2 * channels, dtype=F32),
        [stack(height + 2), stack(height + 2)],
        flags,
        mate,
        mate_edge,
        mate_total,
        own_before,
        own_before_edge,
        both_before[0],
        own,
        own_edge,
        own_total,
        *norm_one,
        pick(weights, 3 - side),
        pick(weights, side),
        acc,
        flops=flops(height, 2),
    )
    before_edge = beside(before_near[:1])
    last = pick(weights, 1 - side)
    bias = row(jnp.tile(bias_one, 2))
    part = shape(near, width, channels)
    sums = shape(2, 8, channels, dtype=F32)
    a1, b1, edges, sums_near = kernel(
        near_kernel,
        [part, part, shape(2, 2, width, channels), sums],
        [stack(near + 2)],
        flags,
        before_near,
        before_edge,
        both_before[1],
        own,
        own_edge,
        own_total,
        mate,
        mate_edge,
        mate_total,
        *norm_one,
        last,
        acc,
        bias,
        flops=flops(near, 1),
    )
    b1_before = later(b1)
    a2, b2, sums_far = kernel(
        far_kernel,
        [part, part, sums],
        [stack(near + 2)],
        flags,
        before_near,
        before_far,
        both_before[1],
        own,
        own_total,
        mate,
        mate_total,
        *norm_one,
        last,
        acc,
        bias,
        flops=flops(near, 1),
    )
    b2_before = later(b2)
    partial = sums_near + sums_far
    totals = partial + beside(partial)
    totals_before = later(totals)
    a1_before = later(a1)
    a2_before = later(a2)
    edges = beside(edges)

    weights = slot_weights(kernel_two, band)
    norm_two = (row(gain_two), row(norm_bias_two))
    acc = kernel(
        local_kernel,
        shape(height + 1, width, 2 * channels, dtype=F32),
        [stack(height + 3), stack(height + 3)],
        flags,
        a1,
        a2,
        b1,
        b2,
        edges,
        totals,
        *norm_two,
        weights[2],
        weights[3],
        flops=flops(height + 1, 2),
    )
    down = jnp.where(band == 0, kernel_down[::-1], kernel_down).reshape(-1, channels)
    residual = pltpu.VMEM((height + 2, width + 8, channels), F32)
    out_shape = shape(height // 2, width // 2, channels)
    b_edge = beside(b1_before[None, :2])
    acc, out_b = kernel(
        second_kernel,
        [shape(height + 1, width, channels, dtype=F32), out_shape],
        [stack(height + 3), residual],
        flags,
        b1_before,
        b2_before,
        b_edge,
        totals_before,
        a1,
        a2,
        edges,
        totals,
        *norm_two,
        weights[1],
        acc,
        row(jnp.tile(bias_two, 2)),
        own,
        mate,
        own_edge,
        mate_edge,
        down,
        row(bias_down),
        flops=flops(height + 1, 1),
    )
    a_edge = beside(a1_before[None, :2])
    thin = weights[0][:, :channels]
    first_near = kernel(
        first_near_kernel,
        part,
        [stack(near + 2)],
        flags,
        a1_before,
        a_edge,
        totals_before,
        a1,
        edges,
        totals,
        *norm_two,
        thin,
        acc,
        own,
        mate,
        own_edge,
        mate_edge,
        flops=flops(near, 1),
    )
    sent, kept = kernel(
        first_far_kernel,
        [out_shape, out_shape],
        [stack(near + 3), residual],
        flags,
        a1_before,
        a2_before,
        totals_before,
        a1,
        a2,
        totals,
        *norm_two,
        thin,
        acc,
        first_near,
        out_b,
        own,
        mate,
        down,
        row(bias_down),
        flops=flops(near, 1),
    )
    received = swapped(sent)
    result = jnp.where(even, jnp.stack([kept, received]), jnp.stack([received, kept]))
    return result[:, None]


def call_sums(x):
    clips, _, _, channels = x.shape
    vmem = pl.BlockSpec(memory_space=pltpu.VMEM)
    return pl.pallas_call(
        sums_kernel,
        out_shape=jax.ShapeDtypeStruct((clips, 8, channels), F32),
        in_specs=[vmem],
        out_specs=vmem,
        cost_estimate=pl.CostEstimate(flops=4 * x.size, bytes_accessed=2 * x.size, transcendentals=0),
    )(x)


def solution(mesh):
    placed = (P("groups", "tm", "rows", None, None),) + (P(),) * 10
    return jax.shard_map(
        local,
        mesh=mesh,
        in_specs=placed,
        out_specs=P("groups", "tm", "rows", None, None),
        check_vma=False,
    )
```

profile of v0, /device:TPU:0, one launch (start us, length us, event | category | flops | bytes accessed | tf_op | source)
XLA Modules:
  0.0 84.5 jit_solution(17405012272830710367)
XLA Ops:
  0.0 2.3 %shard_map.110 = f32[2,8,128]{2,1,0:T(8,128)} custom-call(bf16[2,8,256,128]{3,2,1,0:T(8,128)(2,1)} %bitcast.48), custom_call_target="tpu_custom_call" | custom-call | flops 2097152 | bytes 1048576 | tf_op jit(solution)/shard_map/pallas_call | solution.py:577
  2.3 0.5 collective-permute-start.3
  2.8 0.1 pad_add_fusion.flags
  2.8 1.4 %shard_map.109 = (bf16[8,256,128]{2,1,0:T(8,128)(2,1)S(1)}, bf16[8,256,128]{2,1,0:T(8,128)(2,1)}) custom-call(s32[3]{0:T(128)S(1)} %pad_add_fusion.flags, bf16[2,8,256,128]{3,2,1,0:T(8,128)(2,1)S(1)} %bitcast.49), custom_call_target="tpu_custom_call" | custom-call | bytes 1048576 | tf_op jit(solution)/shard_map/pallas_call | solution.py:300
  4.3 2.6 %collective-permute-start.8 = (bf16[8,256,128]{2,1,0:T(8,128)(2,1)S(1)}, bf16[8,256,128]{2,1,0:T(8,128)(2,1)S(1)}, u32[]{:S(2)}, u32[]{:S(2)}) collective-permute-start(bf16[8,256,128]{2,1,0:T(8,128)(2,1)S(1)} %get-tuple-element.19.x_ref.o_ref.own), channel_id=1, source_target_pairs={{0,4},{2,6},{4,8},{6,10},{8,12},{10,14},{12,0},{14,2},{1,5},{3,7},... | collective-permute-start | bytes 1572872 | tf_op jit(solution)/shard_map/ppermute | solution.py:353
  6.8 0.2 collective-permute-start.6
  7.1 1.5 %collective-permute-start = (bf16[8,256,128]{2,1,0:T(8,128)(2,1)}, bf16[8,256,128]{2,1,0:T(8,128)(2,1)S(1)}, u32[]{:S(2)}, u32[]{:S(2)}) collective-permute-start(bf16[8,256,128]{2,1,0:T(8,128)(2,1)} %get-tuple-element.18), channel_id=1, source_target_pairs={{0,2},{2,0},{4,6},{6,4},{8,10},{10,8},{12,14},{14,12},{1,3},{3,1},... | collective-permute-start | bytes 1572872 | tf_op jit(solution)/shard_map/ppermute | solution.py:350
  8.6 0.1 copy.13
  8.7 1.2 %copy.15 = bf16[3,3,3,128,128]{4,3,1,0,2:T(8,128)(2,1)S(1)} copy(bf16[3,3,3,128,128]{4,3,2,1,0:T(8,128)(2,1)} %param.18) | data formatting | bytes 1769472 | tf_op args[7]
  9.9 0.4 reverse_select_fusion
  10.3 1.7 %pad_slice_fusion.8 = (bf16[4,1152,128]{2,1,0:T(8,128)(2,1)}, bf16[4,1152,128]{2,1,0:T(8,128)(2,1)}) fusion(bf16[3,1152,128]{2,1,0:T(8,128)(2,1)S(1)} %bitcast.80), kind=kLoop, calls=%fused_computation.16 | loop fusion | bytes 3244032 | tf_op jit(solution)/shard_map/slice | solution.py:317
  12.1 1.7 %pad_slice_fusion.6 = (bf16[4,1152,128]{2,1,0:T(8,128)(2,1)}, bf16[4,1152,128]{2,1,0:T(8,128)(2,1)}) fusion(bf16[3,1152,128]{2,1,0:T(8,128)(2,1)S(1)} %bitcast.79), kind=kLoop, calls=%fused_computation.14 | loop fusion | bytes 3244032 | tf_op jit(solution)/shard_map/slice | solution.py:317
  13.8 0.0 collective-permute-done.3
  13.9 0.6 collective-permute-start.4
  14.4 2.7 %fusion.14 = (bf16[1152,256]{1,0:T(8,128)(2,1)S(1)}, bf16[1152,256]{1,0:T(8,128)(2,1)}, bf16[1152,256]{1,0:T(8,128)(2,1)S(1)}, bf16[1152,256]{1,0:T(8,128)(2,1)S(1)}) fusion(bf16[4,1152,128]{2,1,0:T(8,128)(2,1)} %get-tuple-element.39, bf16[4,1152,128]{2,1,0:T(8,128)(2,1)} %get-tuple-element.40), kind=kLoop, calls=%fused_computation.35 | loop fusion | flops 4718592 | bytes 4718592 | tf_op jit(solution)/shard_map/squeeze | solution.py:493
  17.1 4.4 %collective-permute-done.4.tm_ref = f32[8,128]{1,0:T(8,128)S(1)} collective-permute-done((f32[8,128]{1,0:T(8,128)S(1)}, f32[8,128]{1,0:T(8,128)S(1)}, u32[]{:S(2)}, u32[]{:S(2)}) %collective-permute-start.4) | collective-permute-done | bytes 4128 | tf_op jit(solution)/shard_map/ppermute | solution.py:350
  21.5 1.6 %collective-permute-start.5 = (f32[2,8,128]{2,1,0:T(8,128)S(1)}, f32[2,8,128]{2,1,0:T(8,128)S(1)}, u32[]{:S(2)}, u32[]{:S(2)}) collective-permute-start(f32[2,8,128]{2,1,0:T(8,128)S(1)} %pad_maximum_fusion.1), channel_id=1, source_target_pairs={{0,4},{2,6},{4,8},{6,10},{8,12},{10,14},{12,0},{14,2},{1,5},{3,7},... | collective-permute-start | bytes 24584 | tf_op jit(solution)/shard_map/ppermute | solution.py:353
  23.1 1.9 %fusion.7 = (bf16[1152,256]{1,0:T(8,128)(2,1)S(1)}, bf16[1152,256]{1,0:T(8,128)(2,1)S(1)}, bf16[1152,256]{1,0:T(8,128)(2,1)S(1)}, bf16[1152,256]{1,0:T(8,128)(2,1)S(1)}) fusion(s32[]{:T(128)S(6)} %select_n.71, bf16[4,1152,128]{2,1,0:T(8,128)(2,1)} %get-tuple-element.42, bf16[4,1152,128]{2,1,0:T(8,128)(2,1)} %get-tuple-element.41, s32[]{:T(128)S(6)} %select_n.68, ...), kind=kLoop, calls=%fused_computation.27 | loop fusion | flops 4718592 | bytes 4718608 | tf_op jit(solution)/shard_map/jit(dynamic_index_in_dim)/squeeze | solution.py:359
  24.9 0.0 collective-permute-done.m_ref.mate
  25.0 1.6 %collective-permute-start.1 = (bf16[5,256,128]{2,1,0:T(8,128)(2,1)S(1)}, bf16[5,256,128]{2,1,0:T(8,128)(2,1)S(1)}, u32[]{:S(2)}, u32[]{:S(2)}) collective-permute-start(bf16[5,256,128]{2,1,0:T(8,128)(2,1)S(1)} %slice.77), channel_id=1, source_target_pairs={{0,4},{2,6},{4,8},{6,10},{8,12},{10,14},{12,0},{14,2},{1,5},{3,7},... | collective-permute-start | bytes 983048 | tf_op jit(solution)/shard_map/ppermute | solution.py:353
  26.6 0.3 collective-permute-done.5
  26.9 0.1 collective-permute-start.7
  27.0 0.0 collective-permute-done.8.p_ref
  27.0 0.5 collective-permute-start.9
  27.6 0.0 collective-permute-done.6.e_ref.eo_ref
  27.6 2.5 %shard_map.111.in_ref = f32[8,256,256]{2,1,0:T(8,128)S(1)} custom-call(s32[3]{0:T(128)S(1)} %pad_add_fusion.flags, bf16[8,256,128]{2,1,0:T(8,128)(2,1)S(1)} %get-tuple-element.19.x_ref.o_ref.own, bf16[1,256,128]{2,1,0:T(8,128)(2,1)S(1)} %collective-permute-done.6.e_ref.eo_ref, f32[8,128]{1,0:T(8,128)S(1)} %bitcast.53, f32[1,128]{1,0:T(1,128)S(1)} %bitcast.68, ...), custom_call_target="tpu_custom_call" | custom-call | flops 1207959552 | bytes 1184768 | tf_op jit(solution)/shard_map/pallas_call | solution.py:300
  30.2 0.1 collective-permute-start.11
  30.2 6.3 %collective-permute-done.1.p_ref = bf16[5,256,128]{2,1,0:T(8,128)(2,1)S(1)} collective-permute-done((bf16[5,256,128]{2,1,0:T(8,128)(2,1)S(1)}, bf16[5,256,128]{2,1,0:T(8,128)(2,1)S(1)}, u32[]{:S(2)}, u32[]{:S(2)}) %collective-permute-start.1) | collective-permute-done | bytes 327712 | tf_op jit(solution)/shard_map/ppermute | solution.py:353
  36.5 0.0 collective-permute-start.2
  36.5 0.0 collective-permute-done.7.em_ref
  36.5 0.0 collective-permute-done.9.ep_ref
  36.6 0.0 copy-start.10
  36.6 4.0 %shard_map.112.in_ref = f32[8,256,256]{2,1,0:T(8,128)S(1)} custom-call(s32[3]{0:T(128)S(1)} %pad_add_fusion.flags, bf16[8,256,128]{2,1,0:T(8,128)(2,1)S(1)} %collective-permute-done.m_ref.mate, bf16[1,256,128]{2,1,0:T(8,128)(2,1)S(1)} %collective-permute-done.7.em_ref, f32[8,128]{1,0:T(8,128)S(1)} %collective-permute-done.4.tm_ref, ...), custom_call_target="tpu_custom_call" | custom-call | flops 2415919104 | bytes 5059584 | tf_op jit(solution)/shard_map/pallas_call | solution.py:300
  40.6 2.0 %shard_map.113 = (bf16[4,256,128]{2,1,0:T(8,128)(2,1)S(1)}, bf16[4,256,128]{2,1,0:T(8,128)(2,1)S(1)}, bf16[2,2,256,128]{3,2,1,0:T(8,128)(2,1)S(1)}, f32[2,8,128]{2,1,0:T(8,128)S(1)}) custom-call(s32[3]{0:T(128)S(1)} %pad_add_fusion.flags, bf16[5,256,128]{2,1,0:T(8,128)(2,1)S(1)} %collective-permute-done.1.p_ref, ...), custom_call_target="tpu_custom_call" | custom-call | flops 603979776 | bytes 4274176 | tf_op jit(solution)/shard_map/pallas_call | solution.py:300
  42.5 0.0 copy-start.8
  42.6 0.7 collective-permute-start.15
  43.3 0.0 collective-permute-done.11.q_ref
  43.3 1.9 %shard_map.114 = (bf16[4,256,128]{2,1,0:T(8,128)(2,1)S(1)}, bf16[4,256,128]{2,1,0:T(8,128)(2,1)S(1)}, f32[2,8,128]{2,1,0:T(8,128)S(1)}) custom-call(s32[3]{0:T(128)S(1)} %pad_add_fusion.flags, bf16[5,256,128]{2,1,0:T(8,128)(2,1)S(1)} %collective-permute-done.1.p_ref, bf16[3,256,128]{2,1,0:T(8,128)(2,1)S(1)} %collective-permute-done.11.q_ref, ...), custom_call_target="tpu_custom_call" | custom-call | flops 603979776 | bytes 4274176 | tf_op jit(solution)/shard_map/pallas_call | solution.py:300
  45.1 0.0 copy-start.1
  45.2 0.0 copy-start.2
  45.2 0.3 collective-permute-start.13
  45.5 0.3 collective-permute-start.10
  45.9 1.0 %collective-permute-start.16 = (bf16[4,256,128]{2,1,0:T(8,128)(2,1)S(1)}, bf16[4,256,128]{2,1,0:T(8,128)(2,1)S(1)}, u32[]{:S(2)}, u32[]{:S(2)}) collective-permute-start(bf16[4,256,128]{2,1,0:T(8,128)(2,1)S(1)} %get-tuple-element.25.b2), channel_id=1, source_target_pairs={{0,4},{2,6},{4,8},{6,10},{8,12},{10,14},{12,0},{14,2},{1,5},{3,7},... | collective-permute-start | bytes 786440 | tf_op jit(solution)/shard_map/ppermute | solution.py:353
  46.9 3.0 %collective-permute-start.12 = (bf16[4,256,128]{2,1,0:T(8,128)(2,1)S(1)}, bf16[4,256,128]{2,1,0:T(8,128)(2,1)S(1)}, u32[]{:S(2)}, u32[]{:S(2)}) collective-permute-start(bf16[4,256,128]{2,1,0:T(8,128)(2,1)S(1)} %get-tuple-element.21.a2), channel_id=1, source_target_pairs={{0,4},{2,6},{4,8},{6,10},{8,12},{10,14},{12,0},{14,2},{1,5},{3,7},... | collective-permute-start | bytes 786440 | tf_op jit(solution)/shard_map/ppermute | solution.py:353
  49.9 0.0 collective-permute-done.13
  49.9 0.0 collective-permute-start.18
  49.9 3.7 %collective-permute-done.15.b1 = bf16[4,256,128]{2,1,0:T(8,128)(2,1)S(1)} collective-permute-done((bf16[4,256,128]{2,1,0:T(8,128)(2,1)S(1)}, bf16[4,256,128]{2,1,0:T(8,128)(2,1)S(1)}, u32[]{:S(2)}, u32[]{:S(2)}) %collective-permute-start.15) | collective-permute-done | bytes 262176 | tf_op jit(solution)/shard_map/ppermute | solution.py:353
  53.6 0.0 collective-permute-start.14
  53.6 5.6 %collective-permute-done.10.p1 = bf16[4,256,128]{2,1,0:T(8,128)(2,1)S(1)} collective-permute-done((bf16[4,256,128]{2,1,0:T(8,128)(2,1)S(1)}, bf16[4,256,128]{2,1,0:T(8,128)(2,1)S(1)}, u32[]{:S(2)}, u32[]{:S(2)}) %collective-permute-start.10) | collective-permute-done | bytes 262176 | tf_op jit(solution)/shard_map/ppermute | solution.py:353
  59.2 0.0 collective-permute-start.17
  59.2 0.0 collective-permute-done.18.e_ref
  59.2 0.6 collective-permute-start.19
  59.8 4.3 %shard_map.115.in_ref = f32[9,256,256]{2,1,0:T(8,128)S(1)} custom-call(s32[3]{0:T(128)S(1)} %pad_add_fusion.flags, bf16[4,256,128]{2,1,0:T(8,128)(2,1)S(1)} %get-tuple-element.20.a1, bf16[4,256,128]{2,1,0:T(8,128)(2,1)S(1)} %get-tuple-element.21.a2, bf16[4,256,128]{2,1,0:T(8,128)(2,1)S(1)} %get-tuple-element.24.b1, ...), custom_call_target="tpu_custom_call" | custom-call | flops 2717908992 | bytes 2499584 | tf_op jit(solution)/shard_map/pallas_call | solution.py:300
  64.1 6.0 %collective-permute-done.14.tp_ref = f32[2,8,128]{2,1,0:T(8,128)S(1)} collective-permute-done((f32[2,8,128]{2,1,0:T(8,128)S(1)}, f32[2,8,128]{2,1,0:T(8,128)S(1)}, u32[]{:S(2)}, u32[]{:S(2)}) %collective-permute-start.14) | collective-permute-done | bytes 8224 | tf_op jit(solution)/shard_map/ppermute | solution.py:353
  70.1 0.0 collective-permute-done.16.b2
  70.1 0.0 collective-permute-done.17.eb_ref
  70.2 3.8 %shard_map.116 = (f32[9,256,128]{2,1,0:T(8,128)S(1)}, bf16[4,128,128]{2,1,0:T(8,128)(2,1)S(1)}) custom-call(s32[3]{0:T(128)S(1)} %pad_add_fusion.flags, bf16[4,256,128]{2,1,0:T(8,128)(2,1)S(1)} %collective-permute-done.15.b1, bf16[4,256,128]{2,1,0:T(8,128)(2,1)S(1)} %collective-permute-done.16.b2, ...), custom_call_target="tpu_custom_call" | custom-call | flops 1358954496 | bytes 5884416 | tf_op jit(solution)/shard_map/pallas_call | solution.py:300
  74.0 0.0 collective-permute-done.19.ep_ref
  74.0 1.8 %shard_map.117.near_ref = bf16[4,256,128]{2,1,0:T(8,128)(2,1)S(1)} custom-call(s32[3]{0:T(128)S(1)} %pad_add_fusion.flags, bf16[4,256,128]{2,1,0:T(8,128)(2,1)S(1)} %collective-permute-done.10.p1, bf16[1,2,256,128]{3,2,1,0:T(8,128)(2,1)S(1)} %collective-permute-done.19.ep_ref, f32[2,8,128]{2,1,0:T(8,128)S(1)} %collective-permute-done.14.tp_ref, ...), custom_call_target="tpu_custom_call" | custom-call | flops 603979776 | bytes 3589120 | tf_op jit(solution)/shard_map/pallas_call | solution.py:300
  75.8 0.0 collective-permute-done.12.p2
  75.8 2.9 %shard_map.118 = (bf16[4,128,128]{2,1,0:T(8,128)(2,1)S(1)}, bf16[4,128,128]{2,1,0:T(8,128)(2,1)S(1)}) custom-call(s32[3]{0:T(128)S(1)} %pad_add_fusion.flags, bf16[4,256,128]{2,1,0:T(8,128)(2,1)S(1)} %collective-permute-done.10.p1, bf16[4,256,128]{2,1,0:T(8,128)(2,1)S(1)} %collective-permute-done.12.p2, f32[2,8,128]{2,1,0:T(8,128)S(1)} %collective-permute-done.14.tp_ref, ...), custom_call_target="tpu_custom_call" | custom-call | flops 603979776 | bytes 4277760 | tf_op jit(solution)/shard_map/pallas_call | solution.py:300
  78.7 1.6 %collective-permute-start.20 = (bf16[4,128,128]{2,1,0:T(8,128)(2,1)S(1)}, bf16[4,128,128]{2,1,0:T(8,128)(2,1)S(1)}, u32[]{:S(2)}, u32[]{:S(2)}) collective-permute-start(bf16[4,128,128]{2,1,0:T(8,128)(2,1)S(1)} %get-tuple-element.30), channel_id=1, source_target_pairs={{0,2},{2,0},{4,6},{6,4},{8,10},{10,8},{12,14},{14,12},{1,3},{3,1},... | collective-permute-start | bytes 393224 | tf_op jit(solution)/shard_map/ppermute | solution.py:350
  80.3 3.5 %collective-permute-done.20 = bf16[4,128,128]{2,1,0:T(8,128)(2,1)S(1)} collective-permute-done((bf16[4,128,128]{2,1,0:T(8,128)(2,1)S(1)}, bf16[4,128,128]{2,1,0:T(8,128)(2,1)S(1)}, u32[]{:S(2)}, u32[]{:S(2)}) %collective-permute-start.20) | collective-permute-done | bytes 131104 | tf_op jit(solution)/shard_map/ppermute | solution.py:350
  83.8 0.7 maximum_select_fusion
  (39 shorter events, 0.2 us)
Async XLA Ops:
  0.0 2.8 %copy-start = (bf16[2,1,8,256,128]{4,3,2,1,0:T(8,128)(2,1)S(1)}, bf16[2,1,8,256,128]{4,3,2,1,0:T(8,128)(2,1)}, u32[]{:S(2)}) copy-start(bf16[2,1,8,256,128]{4,3,2,1,0:T(8,128)(2,1)} %param.11) | copy-start | bytes 3145732
  0.0 8.6 %copy-start.7 = (bf16[3,3,3,128,128]{4,3,2,1,0:T(8,128)(2,1)S(1)}, bf16[3,3,3,128,128]{4,3,2,1,0:T(8,128)(2,1)}, u32[]{:S(2)}) copy-start(bf16[3,3,3,128,128]{4,3,2,1,0:T(8,128)(2,1)} %param.14) | copy-start | bytes 2654212
  2.3 11.6 %collective-permute-start.3 = (f32[2,8,128]{2,1,0:T(8,128)}, f32[2,8,128]{2,1,0:T(8,128)S(1)}, u32[]{:S(2)}, u32[]{:S(2)}) collective-permute-start(f32[2,8,128]{2,1,0:T(8,128)} %shard_map.110), channel_id=1, source_target_pairs={{0,1},{1,0},{2,3},{3,2},{4,5},{5,4},{6,7},{7,6},{8,9},{9,8},{10,11... | collective-permute-start | bytes 24584 | tf_op jit(solution)/shard_map/ppermute | solution.py:356
  4.3 22.8 %collective-permute-start.8 = (bf16[8,256,128]{2,1,0:T(8,128)(2,1)S(1)}, bf16[8,256,128]{2,1,0:T(8,128)(2,1)S(1)}, u32[]{:S(2)}, u32[]{:S(2)}) collective-permute-start(bf16[8,256,128]{2,1,0:T(8,128)(2,1)S(1)} %get-tuple-element.19.x_ref.o_ref.own), channel_id=1, source_target_pairs={{0,4},{2,6},{4,8},{6,10},{8,12},{10,14},{12,0},{14,2},{1,5},{3,7},... | collective-permute-start | bytes 1572872 | tf_op jit(solution)/shard_map/ppermute | solution.py:353
  6.8 20.8 %collective-permute-start.6 = (bf16[1,256,128]{2,1,0:T(8,128)(2,1)S(1)}, bf16[1,256,128]{2,1,0:T(8,128)(2,1)S(1)}, u32[]{:S(2)}, u32[]{:S(2)}) collective-permute-start(bf16[1,256,128]{2,1,0:T(8,128)(2,1)S(1)} %slice.61), channel_id=1, source_target_pairs={{0,1},{1,0},{2,3},{3,2},{4,5},{5,4},{6,7},{7,6},{8,9},{9,8},{10,11... | collective-permute-start | bytes 196616 | tf_op jit(solution)/shard_map/ppermute | solution.py:356
  7.1 17.9 %collective-permute-start = (bf16[8,256,128]{2,1,0:T(8,128)(2,1)}, bf16[8,256,128]{2,1,0:T(8,128)(2,1)S(1)}, u32[]{:S(2)}, u32[]{:S(2)}) collective-permute-start(bf16[8,256,128]{2,1,0:T(8,128)(2,1)} %get-tuple-element.18), channel_id=1, source_target_pairs={{0,2},{2,0},{4,6},{6,4},{8,10},{10,8},{12,14},{14,12},{1,3},{3,1},... | collective-permute-start | bytes 1572872 | tf_op jit(solution)/shard_map/ppermute | solution.py:350
  12.1 1.8 %copy-start.9 = (f32[2,8,128]{2,1,0:T(8,128)S(1)}, f32[2,8,128]{2,1,0:T(8,128)}, u32[]{:S(2)}) copy-start(f32[2,8,128]{2,1,0:T(8,128)} %shard_map.110) | copy-start | bytes 24580
  13.9 7.6 %collective-permute-start.4 = (f32[8,128]{1,0:T(8,128)S(1)}, f32[8,128]{1,0:T(8,128)S(1)}, u32[]{:S(2)}, u32[]{:S(2)}) collective-permute-start(f32[8,128]{1,0:T(8,128)S(1)} %get-tuple-element.46), channel_id=1, source_target_pairs={{0,2},{2,0},{4,6},{6,4},{8,10},{10,8},{12,14},{14,12},{1,3},{3,1},... | collective-permute-start | bytes 12296 | tf_op jit(solution)/shard_map/ppermute | solution.py:350
  21.5 5.4 %collective-permute-start.5 = (f32[2,8,128]{2,1,0:T(8,128)S(1)}, f32[2,8,128]{2,1,0:T(8,128)S(1)}, u32[]{:S(2)}, u32[]{:S(2)}) collective-permute-start(f32[2,8,128]{2,1,0:T(8,128)S(1)} %pad_maximum_fusion.1), channel_id=1, source_target_pairs={{0,4},{2,6},{4,8},{6,10},{8,12},{10,14},{12,0},{14,2},{1,5},{3,7},... | collective-permute-start | bytes 24584 | tf_op jit(solution)/shard_map/ppermute | solution.py:353
  23.1 4.5 %copy-start.3 = (f32[128]{0:T(128)S(1)}, f32[128]{0:T(128)}, u32[]{:S(2)}) copy-start(f32[128]{0:T(128)} %param.12) | copy-start | bytes 1540
  23.1 4.5 %copy-start.4 = (f32[128]{0:T(128)S(1)}, f32[128]{0:T(128)}, u32[]{:S(2)}) copy-start(f32[128]{0:T(128)} %param.13) | copy-start | bytes 1540
  25.0 11.6 %collective-permute-start.1 = (bf16[5,256,128]{2,1,0:T(8,128)(2,1)S(1)}, bf16[5,256,128]{2,1,0:T(8,128)(2,1)S(1)}, u32[]{:S(2)}, u32[]{:S(2)}) collective-permute-start(bf16[5,256,128]{2,1,0:T(8,128)(2,1)S(1)} %slice.77), channel_id=1, source_target_pairs={{0,4},{2,6},{4,8},{6,10},{8,12},{10,14},{12,0},{14,2},{1,5},{3,7},... | collective-permute-start | bytes 983048 | tf_op jit(solution)/shard_map/ppermute | solution.py:353
  26.9 9.6 %collective-permute-start.7 = (bf16[1,256,128]{2,1,0:T(8,128)(2,1)S(1)}, bf16[1,256,128]{2,1,0:T(8,128)(2,1)S(1)}, u32[]{:S(2)}, u32[]{:S(2)}) collective-permute-start(bf16[1,256,128]{2,1,0:T(8,128)(2,1)S(1)} %slice.80), channel_id=1, source_target_pairs={{0,1},{1,0},{2,3},{3,2},{4,5},{5,4},{6,7},{7,6},{8,9},{9,8},{10,11... | collective-permute-start | bytes 196616 | tf_op jit(solution)/shard_map/ppermute | solution.py:356
  27.0 9.5 %collective-permute-start.9 = (bf16[1,256,128]{2,1,0:T(8,128)(2,1)S(1)}, bf16[1,256,128]{2,1,0:T(8,128)(2,1)S(1)}, u32[]{:S(2)}, u32[]{:S(2)}) collective-permute-start(bf16[1,256,128]{2,1,0:T(8,128)(2,1)S(1)} %slice.81), channel_id=1, source_target_pairs={{0,1},{1,0},{2,3},{3,2},{4,5},{5,4},{6,7},{7,6},{8,9},{9,8},{10,11... | collective-permute-start | bytes 196616 | tf_op jit(solution)/shard_map/ppermute | solution.py:356
  30.2 13.1 %collective-permute-start.11 = (bf16[3,256,128]{2,1,0:T(8,128)(2,1)S(1)}, bf16[3,256,128]{2,1,0:T(8,128)(2,1)S(1)}, u32[]{:S(2)}, u32[]{:S(2)}) collective-permute-start(bf16[3,256,128]{2,1,0:T(8,128)(2,1)S(1)} %slice.83), channel_id=1, source_target_pairs={{0,4},{2,6},{4,8},{6,10},{8,12},{10,14},{12,0},{14,2},{1,5},{3,7},... | collective-permute-start | bytes 589832 | tf_op jit(solution)/shard_map/ppermute | solution.py:353
  36.5 4.0 %collective-permute-start.2 = (bf16[1,256,128]{2,1,0:T(8,128)(2,1)S(1)}, bf16[1,256,128]{2,1,0:T(8,128)(2,1)S(1)}, u32[]{:S(2)}, u32[]{:S(2)}) collective-permute-start(bf16[1,256,128]{2,1,0:T(8,128)(2,1)S(1)} %slice.78), channel_id=1, source_target_pairs={{0,1},{1,0},{2,3},{3,2},{4,5},{5,4},{6,7},{7,6},{8,9},{9,8},{10,11... | collective-permute-start | bytes 196616 | tf_op jit(solution)/shard_map/ppermute | solution.py:356
  36.6 4.0 %copy-start.10 = (f32[128]{0:T(128)S(1)}, f32[128]{0:T(128)}, u32[]{:S(2)}) copy-start(f32[128]{0:T(128)} %param.15) | copy-start | bytes 1540
  42.5 3.2 %copy-start.8 = (bf16[3,3,128,128]{3,2,1,0:T(8,128)(2,1)S(1)}, bf16[3,3,128,128]{3,2,1,0:T(8,128)(2,1)}, u32[]{:S(2)}) copy-start(bf16[3,3,128,128]{3,2,1,0:T(8,128)(2,1)} %param.20) | copy-start | bytes 884740
  42.5 3.3 %copy-start.6 = (bf16[1152,256]{1,0:T(8,128)(2,1)S(1)}, bf16[1152,256]{1,0:T(8,128)(2,1)}, u32[]{:S(2)}) copy-start(bf16[1152,256]{1,0:T(8,128)(2,1)} %get-tuple-element.32) | copy-start | bytes 1769476
  42.6 11.0 %collective-permute-start.15 = (bf16[4,256,128]{2,1,0:T(8,128)(2,1)S(1)}, bf16[4,256,128]{2,1,0:T(8,128)(2,1)S(1)}, u32[]{:S(2)}, u32[]{:S(2)}) collective-permute-start(bf16[4,256,128]{2,1,0:T(8,128)(2,1)S(1)} %get-tuple-element.24.b1), channel_id=1, source_target_pairs={{0,4},{2,6},{4,8},{6,10},{8,12},{10,14},{12,0},{14,2},{1,5},{3,7},... | collective-permute-start | bytes 786440 | tf_op jit(solution)/shard_map/ppermute | solution.py:353
  45.1 14.6 %copy-start.1 = (f32[128]{0:T(128)S(1)}, f32[128]{0:T(128)}, u32[]{:S(2)}) copy-start(f32[128]{0:T(128)} %param.16) | copy-start | bytes 1540
  45.2 14.6 %copy-start.2 = (f32[128]{0:T(128)S(1)}, f32[128]{0:T(128)}, u32[]{:S(2)}) copy-start(f32[128]{0:T(128)} %param.17) | copy-start | bytes 1540
  45.2 4.7 %collective-permute-start.13 = (f32[2,8,128]{2,1,0:T(8,128)S(1)}, f32[2,8,128]{2,1,0:T(8,128)S(1)}, u32[]{:S(2)}, u32[]{:S(2)}) collective-permute-start(f32[2,8,128]{2,1,0:T(8,128)S(1)} %add.51), channel_id=1, source_target_pairs={{0,1},{1,0},{2,3},{3,2},{4,5},{5,4},{6,7},{7,6},{8,9},{9,8},{10,11... | collective-permute-start | bytes 24584 | tf_op jit(solution)/shard_map/ppermute | solution.py:356
  45.5 13.7 %collective-permute-start.10 = (bf16[4,256,128]{2,1,0:T(8,128)(2,1)S(1)}, bf16[4,256,128]{2,1,0:T(8,128)(2,1)S(1)}, u32[]{:S(2)}, u32[]{:S(2)}) collective-permute-start(bf16[4,256,128]{2,1,0:T(8,128)(2,1)S(1)} %get-tuple-element.20.a1), channel_id=1, source_target_pairs={{0,4},{2,6},{4,8},{6,10},{8,12},{10,14},{12,0},{14,2},{1,5},{3,7},... | collective-permute-start | bytes 786440 | tf_op jit(solution)/shard_map/ppermute | solution.py:353
  45.9 24.3 %collective-permute-start.16 = (bf16[4,256,128]{2,1,0:T(8,128)(2,1)S(1)}, bf16[4,256,128]{2,1,0:T(8,128)(2,1)S(1)}, u32[]{:S(2)}, u32[]{:S(2)}) collective-permute-start(bf16[4,256,128]{2,1,0:T(8,128)(2,1)S(1)} %get-tuple-element.25.b2), channel_id=1, source_target_pairs={{0,4},{2,6},{4,8},{6,10},{8,12},{10,14},{12,0},{14,2},{1,5},{3,7},... | collective-permute-start | bytes 786440 | tf_op jit(solution)/shard_map/ppermute | solution.py:353
  46.9 29.0 %collective-permute-start.12 = (bf16[4,256,128]{2,1,0:T(8,128)(2,1)S(1)}, bf16[4,256,128]{2,1,0:T(8,128)(2,1)S(1)}, u32[]{:S(2)}, u32[]{:S(2)}) collective-permute-start(bf16[4,256,128]{2,1,0:T(8,128)(2,1)S(1)} %get-tuple-element.21.a2), channel_id=1, source_target_pairs={{0,4},{2,6},{4,8},{6,10},{8,12},{10,14},{12,0},{14,2},{1,5},{3,7},... | collective-permute-start | bytes 786440 | tf_op jit(solution)/shard_map/ppermute | solution.py:353
  49.9 9.3 %collective-permute-start.18 = (bf16[2,2,256,128]{3,2,1,0:T(8,128)(2,1)S(1)}, bf16[2,2,256,128]{3,2,1,0:T(8,128)(2,1)S(1)}, u32[]{:S(2)}, u32[]{:S(2)}) collective-permute-start(bf16[2,2,256,128]{3,2,1,0:T(8,128)(2,1)S(1)} %get-tuple-element.26), channel_id=1, source_target_pairs={{0,1},{1,0},{2,3},{3,2},{4,5},{5,4},{6,7},{7,6},{8,9},{9,8},{10,11... | collective-permute-start | bytes 786440 | tf_op jit(solution)/shard_map/ppermute | solution.py:356
  53.6 16.5 %collective-permute-start.14 = (f32[2,8,128]{2,1,0:T(8,128)S(1)}, f32[2,8,128]{2,1,0:T(8,128)S(1)}, u32[]{:S(2)}, u32[]{:S(2)}) collective-permute-start(f32[2,8,128]{2,1,0:T(8,128)S(1)} %add.52.t_ref), channel_id=1, source_target_pairs={{0,4},{2,6},{4,8},{6,10},{8,12},{10,14},{12,0},{14,2},{1,5},{3,7},... | collective-permute-start | bytes 24584 | tf_op jit(solution)/shard_map/ppermute | solution.py:353
  59.2 10.9 %collective-permute-start.17 = (bf16[1,2,256,128]{3,2,1,0:T(8,128)(2,1)S(1)}, bf16[1,2,256,128]{3,2,1,0:T(8,128)(2,1)S(1)}, u32[]{:S(2)}, u32[]{:S(2)}) collective-permute-start(bf16[1,2,256,128]{3,2,1,0:T(8,128)(2,1)S(1)} %slice_bitcast_fusion.1), channel_id=1, source_target_pairs={{0,1},{1,0},{2,3},{3,2},{4,5},{5,4},{6,7},{7,6},{8,9},{9,8},{10,11... | collective-permute-start | bytes 393224 | tf_op jit(solution)/shard_map/ppermute | solution.py:356
  59.2 14.8 %collective-permute-start.19 = (bf16[1,2,256,128]{3,2,1,0:T(8,128)(2,1)S(1)}, bf16[1,2,256,128]{3,2,1,0:T(8,128)(2,1)S(1)}, u32[]{:S(2)}, u32[]{:S(2)}) collective-permute-start(bf16[1,2,256,128]{3,2,1,0:T(8,128)(2,1)S(1)} %slice_bitcast_fusion), channel_id=1, source_target_pairs={{0,1},{1,0},{2,3},{3,2},{4,5},{5,4},{6,7},{7,6},{8,9},{9,8},{10,11... | collective-permute-start | bytes 393224 | tf_op jit(solution)/shard_map/ppermute | solution.py:356
  59.8 10.3 %copy-start.11 = (f32[128]{0:T(128)S(1)}, f32[128]{0:T(128)}, u32[]{:S(2)}) copy-start(f32[128]{0:T(128)} %param.19) | copy-start | bytes 1540
  59.8 10.3 %copy-start.5 = (f32[128]{0:T(128)S(1)}, f32[128]{0:T(128)}, u32[]{:S(2)}) copy-start(f32[128]{0:T(128)} %param.21) | copy-start | bytes 1540
  78.7 5.1 %collective-permute-start.20 = (bf16[4,128,128]{2,1,0:T(8,128)(2,1)S(1)}, bf16[4,128,128]{2,1,0:T(8,128)(2,1)S(1)}, u32[]{:S(2)}, u32[]{:S(2)}) collective-permute-start(bf16[4,128,128]{2,1,0:T(8,128)(2,1)S(1)} %get-tuple-element.30), channel_id=1, source_target_pairs={{0,2},{2,0},{4,6},{6,4},{8,10},{10,8},{12,14},{14,12},{1,3},{3,1},... | collective-permute-start | bytes 393224 | tf_op jit(solution)/shard_map/ppermute | solution.py:350
where the time goes:
time: 84.8 us; the launch traced here: 84.5 us
  waiting for transfers between devices  29.8 us (35%)
  Pallas kernels  26.8 us (32%)
  starting transfers between devices  16.7 us (20%)
  other arithmetic  5.84 us (7%)
  local copies, waits for them, and re-layouts  4.97 us (6%)
    pallas_call x9, Pallas kernels, call(): pl.pallas_call(kernel, out_shape=out_shape, in_specs=[pl.BlockSpec(memory...  24.6 us
    ppermute x9, waiting for transfers between devices, later(): return lax.ppermute(v, 'tm', onward)  21.9 us
    ppermute x9, starting transfers between devices, later(): return lax.ppermute(v, 'tm', onward)  10.9 us
    ppermute x3, waiting for transfers between devices, swapped(): return lax.ppermute(v, 'tm', swap)  7.86 us
    ppermute x3, starting transfers between devices, swapped(): return lax.ppermute(v, 'tm', swap)  3.67 us
    slice x2, local copies, waits for them, and re-layouts, slot_weights(): return jnp.concatenate([padded[1:], padded[:-1]], axis=-1)  3.49 us
    squeeze x1, other arithmetic, local(): weights[3]  2.68 us
    pallas_call x1, Pallas kernels, call_sums(): pl.pallas_call(sums_kernel, out_shape=jax.ShapeDtypeStruct((clips, 8, cha...  2.25 us
  transfers between devices with their start and end apart: 21, of which 7 were waited for; matrix products, arithmetic and copies ran while one was open for 12% of the time, Pallas kernels for 26%

commit v1 on v0

v1 whole, which is shorter than its diff:
```python
import functools

import jax
import jax.numpy as jnp
from jax import lax
from jax.experimental import pallas as pl
from jax.experimental.pallas import tpu as pltpu
from jax.sharding import PartitionSpec as P


G = 32
EPSILON = 1e-06
F32 = jnp.float32
BF16 = jnp.bfloat16


def norm_params(totals, gain, bias, cells):
    channels = totals.shape[1]
    size = channels // G
    left = lax.broadcasted_iota(jnp.int32, (channels, channels), 0) // size
    right = lax.broadcasted_iota(jnp.int32, (channels, channels), 1) // size
    same = (left == right).astype(F32)
    grouped = jnp.dot(totals, same, precision=lax.Precision.HIGHEST, preferred_element_type=F32)
    grouped = grouped / (cells * size)
    mean = grouped[0:1]
    inverse = lax.rsqrt(grouped[1:2] - mean * mean + EPSILON)
    return mean, inverse * gain, bias


def keep_params(ref, params):
    for k, value in enumerate(params):
        ref[k : k + 1] = value


def kept_params(ref):
    return ref[0:1], ref[1:2], ref[2:3]


def clear_line(line):
    edge = jnp.zeros((line.shape[0], 8, line.shape[2]), F32)
    line[:, 0:8] = edge
    line[:, line.shape[1] - 8 :] = edge


def fill_row(stack, line, r, values, params):
    mean, scale, bias = params
    width, channels = values.shape
    half = 0.5 * ((values.astype(F32) - mean) * scale + bias)
    normed = half + half * jnp.tanh(half)
    k = r % line.shape[0]
    line[k, 8 : 8 + width] = normed
    stack[r, :, 0:channels] = line[k, 7 : 7 + width].astype(BF16)
    stack[r, :, channels : 2 * channels] = normed.astype(BF16)
    stack[r, :, 2 * channels :] = line[k, 9 : 9 + width].astype(BF16)


def fill_frame(stack, line, values, params):
    for r, value in enumerate(values):
        fill_row(stack, line, r, value(), params)


def close_stack(stack):
    last = stack.shape[0] - 1
    stack[last] = jnp.zeros(stack.shape[1:], BF16)


def taps(stack, weights, start, count):
    rows = [
        jnp.concatenate([stack[r], stack[r + 1], stack[r + 2]], axis=1)
        for r in range(start, start + count)
    ]
    return jnp.dot(jnp.concatenate(rows, axis=0), weights, preferred_element_type=F32)


def steps(first, last):
    total = last - first
    size = 3 if total % 3 == 0 else 2
    return [(r, min(size, last - r)) for r in range(first, last, size)]


def reader(ref, r):
    return lambda: ref[r]


def choose(flags, r, part, k, own, mate):
    def read():
        return jnp.where(flags[1] == 1, jnp.where(flags[0] == 0, own[r], mate[r]), part[k])

    return read


def place_kernel(flags, x_ref, own_ref, other_ref, sem):
    height = own_ref.shape[0]
    side, band = flags[0], flags[2]
    copies = []
    for k, (clip, ref) in enumerate(((side, own_ref), (1 - side, other_ref))):
        for r in range(height):
            row = jnp.where(band == 0, height - 1 - r, r)
            copies.append(pltpu.make_async_copy(x_ref.at[clip, row], ref.at[r], sem.at[k, r]))
    for copy in copies:
        copy.start()
    for copy in copies:
        copy.wait()


def weights_kernel(slots, flags, *refs):
    k_ref, *outs = refs
    channels = k_ref.shape[-1]
    band = flags[2]
    for slot, out in zip(slots(flags), outs):
        for f in range(out.shape[1] // channels):
            frame = slot - f
            known = jnp.logical_and(frame >= 0, frame <= 2)
            frame = jnp.clip(frame, 0, 2)
            for a in range(3):
                tap = jnp.where(band == 0, 2 - a, a)
                for b in range(3):
                    k = (3 * a + b) * channels
                    block = jnp.where(known, k_ref[tap, b, frame], jnp.zeros((), BF16))
                    out[k : k + channels, f * channels : (f + 1) * channels] = block


def sums_kernel(own_ref, other_ref, out_ref):
    height, width, channels = own_ref.shape
    for c, x_ref in enumerate((own_ref, other_ref)):
        total = jnp.zeros((8, channels), F32)
        square = jnp.zeros((8, channels), F32)
        for r in range(height):
            v = x_ref[r].astype(F32).reshape(width // 8, 8, channels)
            total += jnp.sum(v, axis=0)
            square += jnp.sum(v * v, axis=0)
        out_ref[c, 0:1] = jnp.sum(total, axis=0, keepdims=True)
        out_ref[c, 1:2] = jnp.sum(square, axis=0, keepdims=True)
        out_ref[c, 2:8] = jnp.zeros((6, channels), F32)


def own_kernel(cells, flags, x_ref, e_ref, t_ref, g_ref, c_ref, w_ref, acc_ref, stack, line):
    height, width, _ = x_ref.shape
    clear_line(line)
    params = norm_params(t_ref[...], g_ref[...], c_ref[...], cells)
    fill_frame(stack, line, [reader(e_ref, 0)] + [reader(x_ref, r) for r in range(height)], params)
    close_stack(stack)
    for start, count in steps(0, height):
        part = taps(stack, w_ref[...], start, count)
        acc_ref[start : start + count] = part.reshape(count, width, -1)


def mates_kernel(cells, flags, m_ref, tm_ref, p_ref, e_ref, tp_ref, o_ref, eo_ref, to_ref, tq_ref, g_ref, c_ref, wm_ref, wp_ref, in_ref, acc_ref, last_ref, xm, xp, line):
    height, width, _ = m_ref.shape
    first, even = flags[1] == 1, flags[0] == 0
    clear_line(line)
    params = norm_params(tm_ref[...], g_ref[...], c_ref[...], cells)
    fill_frame(xm, line, [reader(e_ref, 0)] + [reader(m_ref, r) for r in range(height)], params)
    close_stack(xm)
    start_totals = jnp.where(even, to_ref[...], tm_ref[...])
    totals = jnp.where(first, start_totals, tp_ref[...])
    params = norm_params(totals, g_ref[...], c_ref[...], cells)
    values = [lambda: jnp.where(first, jnp.where(even, eo_ref[0], e_ref[0]), e_ref[1])]
    values += [choose(flags, r, p_ref, r, o_ref, m_ref) for r in range(height)]
    fill_frame(xp, line, values, params)
    close_stack(xp)
    for start, count in steps(0, height):
        part = taps(xm, wm_ref[...], start, count) + taps(xp, wp_ref[...], start, count)
        acc_ref[start : start + count] = in_ref[start : start + count] + part.reshape(count, width, -1)
    totals = jnp.where(first, start_totals, tq_ref[...])
    keep_params(last_ref, norm_params(totals, g_ref[...], c_ref[...], cells))


def hidden_rows(stack, w_ref, in_ref, bias_ref, first, a_ref, b_ref, sum_ref):
    rows, width, channels = a_ref.shape
    both = 2 * channels
    total = jnp.zeros((8, both), F32)
    square = jnp.zeros((8, both), F32)
    for start, count in steps(0, rows):
        part = taps(stack, w_ref[...], start, count).reshape(count, width, both)
        begin = first + start
        hidden = (in_ref[begin : begin + count] + part + bias_ref[...]).astype(BF16)
        a_ref[start : start + count] = hidden[:, :, :channels]
        b_ref[start : start + count] = hidden[:, :, channels:]
        wide = hidden.astype(F32).reshape(count * width // 8, 8, both)
        total += jnp.sum(wide, axis=0)
        square += jnp.sum(wide * wide, axis=0)
    total = jnp.sum(total, axis=0, keepdims=True)
    square = jnp.sum(square, axis=0, keepdims=True)
    for k in range(2):
        sum_ref[k, 0:1] = total[:, k * channels : (k + 1) * channels]
        sum_ref[k, 1:2] = square[:, k * channels : (k + 1) * channels]
        sum_ref[k, 2:8] = jnp.zeros((6, channels), F32)


def near_kernel(cells, flags, p_ref, ep_ref, n_ref, o_ref, eo_ref, m_ref, e_ref, w_ref, in_ref, bias_ref, a_ref, b_ref, edge_ref, sum_ref, stack, line):
    clear_line(line)
    rows = a_ref.shape[0]
    values = [choose(flags, 0, ep_ref, 0, eo_ref, e_ref)]
    values += [choose(flags, r, p_ref, r, o_ref, m_ref) for r in range(rows + 1)]
    fill_frame(stack, line, values, kept_params(n_ref))
    hidden_rows(stack, w_ref, in_ref, bias_ref, 0, a_ref, b_ref, sum_ref)
    edge_ref[0] = a_ref[0:2]
    edge_ref[1] = b_ref[0:2]


def far_kernel(cells, flags, p_ref, q_ref, n_ref, o_ref, m_ref, w_ref, in_ref, bias_ref, near_ref, part_ref, a_ref, b_ref, c_ref, sum_ref, stack, line, held):
    clear_line(line)
    height, near = o_ref.shape[0], p_ref.shape[0]
    rows, early = b_ref.shape[0], near_ref.shape[0]
    values = []
    for r in range(height - rows - 1, height):
        part, k = (p_ref, r) if r < near else (q_ref, r - near)
        values.append(choose(flags, r, part, k, o_ref, m_ref))
    fill_frame(stack, line, values, kept_params(n_ref))
    close_stack(stack)
    hidden_rows(stack, w_ref, in_ref, bias_ref, height - rows, held, b_ref, sum_ref)
    sum_ref[...] += part_ref[...]
    whole = a_ref.shape[0]
    a_ref[0:early] = near_ref[...]
    a_ref[early:] = held[0 : whole - early]
    c_ref[...] = held[whole - early :]


def halves(edge, k, near, far):
    rows = [lambda: edge[k, 1], lambda: edge[k, 0]]
    rows += [reader(near, r) for r in range(near.shape[0])]
    return rows + [reader(far, r) for r in range(far.shape[0])]


def local_kernel(cells, flags, a1, a2, b1, b2, e_ref, t_ref, g_ref, c_ref, wa_ref, wb_ref, acc_ref, xa, xb, line):
    out_rows, width, _ = acc_ref.shape
    clear_line(line)
    for k, (stack, near, far) in enumerate(((xa, a1, a2), (xb, b1, b2))):
        params = norm_params(t_ref[k], g_ref[...], c_ref[...], cells)
        fill_frame(stack, line, halves(e_ref, k, near, far), params)
        close_stack(stack)
    for start, count in steps(0, out_rows):
        part = taps(xa, wa_ref[...], start, count) + taps(xb, wb_ref[...], start, count)
        acc_ref[start : start + count] = part.reshape(count, width, -1)


def either(flags, first, other):
    return lambda: jnp.where(flags[1] == 1, first(), other())


def residual_row(raw, branch):
    return (raw.astype(F32) + branch).astype(BF16)


def put_row(res, r, value):
    res[r, 0 : value.shape[0], :] = value.astype(F32)


def down_rows(flags, res, wd_ref, bd_ref, first, last):
    half = (res.shape[1] - 8) // 2
    band = flags[2]
    rows = []
    for i in range(first, last):
        cols = [
            res[2 * i + a + band, pl.ds(b, half, stride=2), :].astype(BF16)
            for a in range(3)
            for b in range(3)
        ]
        rows.append(jnp.concatenate(cols, axis=1))
    out = jnp.dot(jnp.concatenate(rows, axis=0), wd_ref[...], preferred_element_type=F32)
    out = (out + bd_ref[...]).astype(BF16)
    return out.reshape(last - first, half, -1)


def second_kernel(cells, flags, b1, b2, eb_ref, tp_ref, a1, a2, e_ref, t_ref, g_ref, c_ref, w_ref, in_ref, bias_ref, own, mate, eo_ref, em_ref, wd_ref, bd_ref, acc_ref, out_ref, last_ref, stack, line, res):
    out_rows, width, channels = acc_ref.shape
    height = out_rows - 1
    even = flags[0] == 0
    clear_line(line)
    params = norm_params(jnp.where(flags[1] == 1, t_ref[0], tp_ref[1]), g_ref[...], c_ref[...], cells)
    values = [
        either(flags, f, o) for f, o in zip(halves(e_ref, 0, a1, a2), halves(eb_ref, 0, b1, b2))
    ]
    fill_frame(stack, line, values, params)
    close_stack(stack)
    res[:, width:, :] = jnp.zeros((res.shape[0], res.shape[1] - width, channels), F32)
    res[out_rows] = jnp.zeros(res.shape[1:], F32)
    for start, count in steps(0, out_rows):
        part = taps(stack, w_ref[...], start, count).reshape(count, width, 2 * channels)
        branch = in_ref[start : start + count] + part + bias_ref[...]
        acc_ref[start : start + count] = branch[:, :, :channels]
        for k in range(count):
            r = start + k - 1
            raw = jnp.where(even, mate[r], own[r]) if r >= 0 else jnp.where(even, em_ref[0], eo_ref[0])
            put_row(res, r + 1, residual_row(raw, branch[k, :, channels:]))
    out_ref[...] = down_rows(flags, res, wd_ref, bd_ref, 0, height // 2)
    params = norm_params(jnp.where(flags[1] == 1, t_ref[0], tp_ref[0]), g_ref[...], c_ref[...], cells)
    keep_params(last_ref, params)


def route(flags, out, other_ref, first, send_ref, keep_ref):
    even = flags[0] == 0
    other = other_ref[first : first + out.shape[0]]
    send_ref[...] = jnp.where(even, other, out)
    keep_ref[...] = jnp.where(even, out, other)


def first_near_kernel(cells, flags, p1, ep_ref, n_ref, a1, e_ref, w_ref, in_ref, own, mate, eo_ref, em_ref, other_ref, wd_ref, bd_ref, out_ref, send_ref, keep_ref, stack, line, res):
    rows, width, channels = out_ref.shape
    even = flags[0] == 0
    clear_line(line)
    firsts = [lambda: e_ref[0, 1], lambda: e_ref[0, 0]] + [reader(a1, r) for r in range(rows)]
    others = [lambda: ep_ref[0, 1], lambda: ep_ref[0, 0]] + [reader(p1, r) for r in range(rows)]
    values = [either(flags, f, o) for f, o in zip(firsts, others)]
    fill_frame(stack, line, values, kept_params(n_ref))
    res[:, width:, :] = jnp.zeros((res.shape[0], res.shape[1] - width, channels), F32)
    for start, count in steps(0, rows):
        part = taps(stack, w_ref[...], start, count).reshape(count, width, channels)
        branch = in_ref[start : start + count] + part
        for k in range(count):
            r = start + k - 1
            raw = jnp.where(even, own[r], mate[r]) if r >= 0 else jnp.where(even, eo_ref[0], em_ref[0])
            value = residual_row(raw, branch[k])
            out_ref[r + 1] = value
            put_row(res, r + 1, value)
    out = down_rows(flags, res, wd_ref, bd_ref, 0, send_ref.shape[0])
    route(flags, out, other_ref, 0, send_ref, keep_ref)


def first_far_kernel(cells, flags, p1, p2, n_ref, a1, a2, w_ref, in_ref, near_ref, other_ref, own, mate, wd_ref, bd_ref, send_ref, keep_ref, stack, line, res):
    out_rows, width, channels = in_ref.shape
    height = out_rows - 1
    half = p1.shape[0]
    done = near_ref.shape[0]
    even = flags[0] == 0
    clear_line(line)
    values = []
    for r in range(done - 2, height):
        f, o, k = (a1, p1, r) if r < half else (a2, p2, r - half)
        values.append(either(flags, reader(f, k), reader(o, k)))
    fill_frame(stack, line, values, kept_params(n_ref))
    close_stack(stack)
    first = height // 2 - send_ref.shape[0]
    res[:, width:, :] = jnp.zeros((res.shape[0], res.shape[1] - width, channels), F32)
    res[out_rows] = jnp.zeros(res.shape[1:], F32)
    for r in range(2 * first, done):
        put_row(res, r, near_ref[r])
    for start, count in steps(0, out_rows - done):
        part = taps(stack, w_ref[...], start, count).reshape(count, width, channels)
        branch = in_ref[done + start : done + start + count] + part
        for k in range(count):
            r = done + start + k - 1
            put_row(res, r + 1, residual_row(jnp.where(even, own[r], mate[r]), branch[k]))
    out = down_rows(flags, res, wd_ref, bd_ref, first, height // 2)
    route(flags, out, other_ref, first, send_ref, keep_ref)


def join_kernel(flags, kept1, kept2, got1, got2, out_ref):
    rows = out_ref.shape[1]
    for clip, parts in ((flags[0], (kept1, kept2)), (1 - flags[0], (got1, got2))):
        for i in range(rows):
            part, k = (parts[0], i) if i < kept1.shape[0] else (parts[1], i - kept1.shape[0])
            out_ref[clip, jnp.where(flags[2] == 0, rows - 1 - i, i)] = part[k]


def call(kernel, out_shape, scratch, flags, *args, flops=0):
    vmem = pl.BlockSpec(memory_space=pltpu.VMEM)
    several = isinstance(out_shape, (list, tuple))
    moved = sum(a.size * a.dtype.itemsize for a in args)
    return pl.pallas_call(
        kernel,
        out_shape=out_shape,
        in_specs=[pl.BlockSpec(memory_space=pltpu.SMEM)] + [vmem] * len(args),
        out_specs=[vmem] * len(out_shape) if several else vmem,
        scratch_shapes=scratch,
        cost_estimate=pl.CostEstimate(flops=flops, bytes_accessed=moved, transcendentals=0),
        compiler_params=pltpu.CompilerParams(vmem_limit_bytes=32 << 20),
    )(flags, *args)


def call_place(flags, x, frame):
    height = frame.shape[0]
    vmem = pl.BlockSpec(memory_space=pltpu.VMEM)
    return pl.pallas_call(
        place_kernel,
        out_shape=[frame, frame],
        in_specs=[pl.BlockSpec(memory_space=pltpu.SMEM), pl.BlockSpec(memory_space=pl.ANY)],
        out_specs=[vmem, vmem],
        scratch_shapes=[pltpu.SemaphoreType.DMA((2, height))],
        cost_estimate=pl.CostEstimate(flops=0, bytes_accessed=4 * x.size, transcendentals=0),
    )(flags, x)


def call_sums(own, other):
    channels = own.shape[-1]
    vmem = pl.BlockSpec(memory_space=pltpu.VMEM)
    return pl.pallas_call(
        sums_kernel,
        out_shape=jax.ShapeDtypeStruct((2, 8, channels), F32),
        in_specs=[vmem, vmem],
        out_specs=vmem,
        cost_estimate=pl.CostEstimate(flops=8 * own.size, bytes_accessed=4 * own.size, transcendentals=0),
    )(own, other)


def slots_one(flags):
    side = flags[0]
    return 2 + side, 3 - side, side, 1 - side


def slots_two(flags):
    return 2, 3, 1, 0


def turned(value, band):
    return jnp.where(band == 0, value[::-1], value)


def local(
    frames_in,
    gain_one,
    norm_bias_one,
    kernel_one,
    bias_one,
    gain_two,
    norm_bias_two,
    kernel_two,
    bias_two,
    kernel_down,
    bias_down,
):
    x = frames_in[:, 0]
    clips, height, width, channels = x.shape
    count = lax.axis_size("tm")
    bands = lax.axis_size("rows")
    assert clips == 2 and bands == 2 and count % 2 == 0 and height % 8 == 0
    cells = height * bands * width
    near = 3 * height // 8
    tail = height // TAIL
    position = lax.axis_index("tm")
    band = lax.axis_index("rows")
    side = position % 2
    flags = jnp.stack([side, (position < 2).astype(jnp.int32), band]).astype(jnp.int32)
    swap = [(i, i ^ 1) for i in range(count)]
    across = [(0, 1), (1, 0)]

    def onward(name, turn):
        wrap = name not in OPEN
        pairs = [(i, (i ^ turn) + 2) for i in range(count)]
        return [(i, j % count) for i, j in pairs if wrap or j < count]

    def swapped(v):
        return lax.ppermute(v, "tm", swap)

    def later(v, name):
        return lax.ppermute(v, "tm", onward(name, 0))

    def crossed(v, name):
        return lax.ppermute(v, "tm", onward(name, 1))

    def beside(v):
        return lax.ppermute(v, "rows", across)

    def row(v):
        return v.reshape(1, -1)

    def stack(rows):
        line = pltpu.VMEM((2, width + 16, channels), F32)
        return [pltpu.VMEM((rows, width, 3 * channels), BF16), line]

    def flops(rows, slots):
        return 2 * rows * width * 9 * channels * 2 * channels * slots

    def shape(*dims, dtype=BF16):
        return jax.ShapeDtypeStruct(dims, dtype)

    def kernel(body, *rest, **options):
        return call(functools.partial(body, cells), *rest, **options)

    def weights(slots, kernel, last):
        shapes = [shape(9 * channels, n * channels) for n in (2, 2, 2, last)]
        return call(functools.partial(weights_kernel, slots), shapes, [], flags, kernel)

    own, other = call_place(flags, x, shape(height, width, channels))
    own_on = later(own, "own_on")
    mate = swapped(other)
    partial = call_sums(own, other)
    totals = partial + beside(partial)
    own_total, other_total = totals[0], totals[1]
    own_on_total = later(own_total, "own_sums")
    cross_total = crossed(other_total, "cross_sums")
    mate_total = swapped(other_total)
    own_edge = beside(own[:1])
    split = near + 1
    cross_near = crossed(other[:split], "cross1")
    cross_far = crossed(other[split:], "cross2")

    w_own, w_mate, w_own_on, w_cross = weights(slots_one, kernel_one, 2)
    norm_one = (row(gain_one), row(norm_bias_one))
    sums = shape(2, 8, channels, dtype=F32)
    params = shape(8, channels, dtype=F32)
    acc_shape = shape(height, width, 2 * channels, dtype=F32)
    acc = kernel(
        own_kernel,
        acc_shape,
        stack(height + 2),
        flags,
        own,
        own_edge,
        own_total,
        *norm_one,
        w_own,
        flops=flops(height, 1),
    )
    pair_edge = beside(jnp.concatenate([mate[:1], own_on[:1]]))
    acc, cross_params = kernel(
        mates_kernel,
        [acc_shape, params],
        stack(height + 2)[:1] + stack(height + 2),
        flags,
        mate,
        mate_total,
        own_on,
        pair_edge,
        own_on_total,
        own,
        own_edge,
        own_total,
        cross_total,
        *norm_one,
        w_mate,
        w_own_on,
        acc,
        flops=flops(height, 2),
    )
    cross_edge = beside(cross_near[:1])
    bias = row(jnp.tile(bias_one, 2))
    part = shape(near, width, channels)
    rest = shape(height - near, width, channels)
    early = shape(height - tail, width, channels)
    a_near, b1, edges, sums_near = kernel(
        near_kernel,
        [part, part, shape(2, 2, width, channels), sums],
        stack(near + 2),
        flags,
        cross_near,
        cross_edge,
        cross_params,
        own,
        own_edge,
        mate,
        pair_edge,
        w_cross,
        acc,
        bias,
        flops=flops(near, 1),
    )
    b1_on = later(b1, "b_on1")
    a1, b2, a2, partial = kernel(
        far_kernel,
        [early, rest, shape(tail, width, channels), sums],
        stack(height - near + 2) + [pltpu.VMEM(rest.shape, BF16)],
        flags,
        cross_near,
        cross_far,
        cross_params,
        own,
        mate,
        w_cross,
        acc,
        bias,
        a_near,
        sums_near,
        flops=flops(height - near, 1),
    )
    b2_on = later(b2, "b_on2")
    totals = partial + beside(partial)
    totals_on = later(totals, "hsums_on")
    a1_on = later(a1, "a_on1")
    a2_on = later(a2, "a_on2")
    edges = beside(edges)

    w_a, w_b, w_b_on, w_a_on = weights(slots_two, kernel_two, 1)
    norm_two = (row(gain_two), row(norm_bias_two))
    acc = kernel(
        local_kernel,
        shape(height + 1, width, 2 * channels, dtype=F32),
        stack(height + 3)[:1] + stack(height + 3),
        flags,
        a1,
        a2,
        b1,
        b2,
        edges,
        totals,
        *norm_two,
        w_a,
        w_b,
        flops=flops(height + 1, 2),
    )
    down = turned(kernel_down, band).reshape(-1, channels)
    residual = [pltpu.VMEM((height + 2, width + 8, channels), F32)]
    b_edge = beside(b1_on[None, :2])
    acc, out_b, a_params = kernel(
        second_kernel,
        [
            shape(height + 1, width, channels, dtype=F32),
            shape(height // 2, width // 2, channels),
            params,
        ],
        stack(height + 3) + residual,
        flags,
        b1_on,
        b2_on,
        b_edge,
        totals_on,
        a1,
        a2,
        edges,
        totals,
        *norm_two,
        w_b_on,
        acc,
        row(jnp.tile(bias_two, 2)),
        own,
        mate,
        own_edge,
        pair_edge,
        down,
        row(bias_down),
        flops=flops(height + 1, 1),
    )
    a_edge = beside(a1_on[None, :2])
    ready = height - tail
    early_out = (ready - 2) // 2
    late_out = height // 2 - early_out
    half_out = shape(early_out, width // 2, channels)
    last_out = shape(late_out, width // 2, channels)
    first_near, sent1, kept1 = kernel(
        first_near_kernel,
        [shape(ready, width, channels), half_out, half_out],
        stack(ready + 2) + residual,
        flags,
        a1_on,
        a_edge,
        a_params,
        a1,
        edges,
        w_a_on,
        acc,
        own,
        mate,
        own_edge,
        pair_edge,
        out_b,
        down,
        row(bias_down),
        flops=flops(ready, 1),
    )
    got1 = swapped(sent1)
    sent2, kept2 = kernel(
        first_far_kernel,
        [last_out, last_out],
        stack(tail + 3) + residual,
        flags,
        a1_on,
        a2_on,
        a_params,
        a1,
        a2,
        w_a_on,
        acc,
        first_near,
        out_b,
        own,
        mate,
        down,
        row(bias_down),
        flops=flops(tail + 1, 1),
    )
    got2 = swapped(sent2)
    result = call(
        join_kernel,
        shape(2, height // 2, width // 2, channels),
        [],
        flags,
        kept1,
        kept2,
        got1,
        got2,
    )
    return result[:, None]


OPEN = ()
TAIL = 2


def solution(mesh):
    placed = (P("groups", "tm", "rows", None, None),) + (P(),) * 10
    return jax.shard_map(
        local,
        mesh=mesh,
        in_specs=placed,
        out_specs=P("groups", "tm", "rows", None, None),
        check_vma=False,
    )
```

time: 84.8 us -> 84.5 us (level)
  Pallas kernels: 26.8 us -> 32.5 us
  other arithmetic: 5.84 us -> 1.44 us
  local copies, waits for them, and re-layouts: 4.97 us -> 2 us
  starting transfers between devices: 16.7 us -> 19.2 us
  waiting for transfers between devices: 29.8 us -> 28.8 us
    squeeze x2 -> x0, other arithmetic: 4.55 us -> none  [the longest x1 2.68 us: local(): weights[3]]
    pallas_call x1 -> x2, Pallas kernels: 2.25 us -> 5.24 us  [the longest x1 3.15 us: call_place(): pl.pallas_call(place_kernel, out_shape=[frame, frame], in_specs=[pl.Block...]
    pallas_call x9 -> x11, Pallas kernels: 24.6 us -> 27.2 us  [call(): pl.pallas_call(kernel, out_shape=out_shape, in_specs=[pl.BlockSpec(memory...]
    slice x8 -> x4, local copies, waits for them, and re-layouts: 3.56 us -> 1.08 us  [the longest x1 1.06 us: local(): cross_far = crossed(other[split:], 'cross2')]
    ppermute x3 -> x4, waiting for transfers between devices: 7.86 us -> 5.64 us  [swapped(): return lax.ppermute(v, 'tm', swap)]
    ppermute x3 -> x4, starting transfers between devices: 3.67 us -> 5.5 us  [swapped(): return lax.ppermute(v, 'tm', swap)]
    ppermute x9 -> x10, starting transfers between devices: 10.9 us -> 12.3 us  [the longest x7 8.21 us: later(): return lax.ppermute(v, 'tm', onward(name, 0))]
    unnamed x26 -> x24, local copies, waits for them, and re-layouts: 1.36 us -> 0.05 us
  transfers between devices with their start and end apart: 21 -> 22, of which waited for: 7 -> 7; matrix products, arithmetic and copies ran while one was open for 12% -> 3% of each run, Pallas kernels for 26% -> 28%
where the time goes in v1:
time: 84.5 us; the launch traced here: 84.2 us
  Pallas kernels  32.5 us (38%)
  waiting for transfers between devices  28.8 us (34%)
  starting transfers between devices  19.2 us (23%)
  local copies, waits for them, and re-layouts  2 us (2%)
  other arithmetic  1.44 us (2%)
    pallas_call x11, Pallas kernels, call(): pl.pallas_call(kernel, out_shape=out_shape, in_specs=[pl.BlockSpec(memory...  27.2 us
    ppermute x7, waiting for transfers between devices, later(): return lax.ppermute(v, 'tm', onward(name, 0))  20.5 us
    ppermute x7, starting transfers between devices, later(): return lax.ppermute(v, 'tm', onward(name, 0))  8.21 us
    ppermute x4, waiting for transfers between devices, swapped(): return lax.ppermute(v, 'tm', swap)  5.64 us
    ppermute x4, starting transfers between devices, swapped(): return lax.ppermute(v, 'tm', swap)  5.5 us
    ppermute x3, starting transfers between devices, crossed(): return lax.ppermute(v, 'tm', onward(name, 1))  4.1 us
    pallas_call x1, Pallas kernels, call_place(): pl.pallas_call(place_kernel, out_shape=[frame, frame], in_specs=[pl.Block...  3.15 us
    ppermute x3, waiting for transfers between devices, crossed(): return lax.ppermute(v, 'tm', onward(name, 1))  2.6 us
  transfers between devices with their start and end apart: 22, of which 7 were waited for; matrix products, arithmetic and copies ran while one was open for 3% of the time, Pallas kernels for 28%

profile of v1, /device:TPU:0, one launch (start us, length us, event | category | flops | bytes accessed | tf_op | source)
XLA Modules:
  0.0 84.2 jit_solution(6396044771090903579)
XLA Ops:
  0.0 0.7 pad_add_fusion.flags
  0.7 3.2 %shard_map.109 = (bf16[8,256,128]{2,1,0:T(8,128)(2,1)}, bf16[8,256,128]{2,1,0:T(8,128)(2,1)}) custom-call(s32[3]{0:T(128)} %pad_add_fusion.flags, bf16[2,8,256,128]{3,2,1,0:T(8,128)(2,1)} %bitcast.40), custom_call_target="tpu_custom_call" | custom-call | bytes 2097152 | tf_op jit(solution)/shard_map/pallas_call | solution.py:375
  3.8 0.0 copy-start.7
  3.9 0.0 copy-start.8
  3.9 3.1 %collective-permute-start.2 = (bf16[8,256,128]{2,1,0:T(8,128)(2,1)}, bf16[8,256,128]{2,1,0:T(8,128)(2,1)S(1)}, u32[]{:S(2)}, u32[]{:S(2)}) collective-permute-start(bf16[8,256,128]{2,1,0:T(8,128)(2,1)} %get-tuple-element.33.other_ref), channel_id=1, source_target_pairs={{0,2},{2,0},{4,6},{6,4},{8,10},{10,8},{12,14},{14,12},{1,3},{3,1},... | collective-permute-start | bytes 1572872 | tf_op jit(solution)/shard_map/ppermute | solution.py:444
  6.9 1.6 %collective-permute-start.5 = (bf16[8,256,128]{2,1,0:T(8,128)(2,1)}, bf16[8,256,128]{2,1,0:T(8,128)(2,1)S(1)}, u32[]{:S(2)}, u32[]{:S(2)}) collective-permute-start(bf16[8,256,128]{2,1,0:T(8,128)(2,1)} %get-tuple-element.34.own_ref.x_ref.o_ref.own), channel_id=1, source_target_pairs={{0,4},{2,6},{4,8},{6,10},{8,12},{10,14},{12,0},{14,2},{1,5},{3,7},... | collective-permute-start | bytes 1572872 | tf_op jit(solution)/shard_map/ppermute | solution.py:447
  8.5 2.1 %shard_map.110 = f32[2,8,128]{2,1,0:T(8,128)} custom-call(bf16[8,256,128]{2,1,0:T(8,128)(2,1)} %get-tuple-element.34.own_ref.x_ref.o_ref.own, bf16[8,256,128]{2,1,0:T(8,128)(2,1)} %get-tuple-element.33.other_ref), custom_call_target="tpu_custom_call" | custom-call | flops 2097152 | bytes 1048576 | tf_op jit(solution)/shard_map/pallas_call | solution.py:388
  10.6 0.0 collective-permute-start.3
  10.6 0.8 %slice.36 = bf16[1,256,128]{2,1,0:T(8,128)(2,1)S(1)} slice(bf16[8,256,128]{2,1,0:T(8,128)(2,1)} %get-tuple-element.34.own_ref.x_ref.o_ref.own), slice={[0:1], [0:256], [0:128]} | slice | bytes 131072 | tf_op jit(solution)/shard_map/slice | solution.py:484
  11.4 0.5 collective-permute-start.8
  12.0 1.1 %fusion = (bf16[4,256,128]{2,1,0:T(8,128)(2,1)S(1)}, bf16[4,256,128]{2,1,0:T(8,128)(2,1)S(1)}) fusion(bf16[8,256,128]{2,1,0:T(8,128)(2,1)} %get-tuple-element.33.other_ref), kind=kLoop, calls=%fused_computation.7 | loop fusion | bytes 1048576 | tf_op jit(solution)/shard_map/slice | solution.py:487
  13.0 1.6 %collective-permute-start = (bf16[4,256,128]{2,1,0:T(8,128)(2,1)S(1)}, bf16[4,256,128]{2,1,0:T(8,128)(2,1)S(1)}, u32[]{:S(2)}, u32[]{:S(2)}) collective-permute-start(bf16[4,256,128]{2,1,0:T(8,128)(2,1)S(1)} %get-tuple-element.62), channel_id=1, source_target_pairs={{0,6},{2,4},{4,10},{6,8},{8,14},{10,12},{12,2},{14,0},{1,7},{3,5},... | collective-permute-start | bytes 786440 | tf_op jit(solution)/shard_map/ppermute | solution.py:450
  14.6 1.1 %shard_map.111 = (bf16[1152,256]{1,0:T(8,128)(2,1)S(1)}, bf16[1152,256]{1,0:T(8,128)(2,1)S(1)}, bf16[1152,256]{1,0:T(8,128)(2,1)S(1)}, bf16[1152,256]{1,0:T(8,128)(2,1)S(1)}) custom-call(s32[3]{0:T(128)S(1)} %copy-done.3, bf16[3,3,3,128,128]{4,3,2,1,0:T(8,128)(2,1)S(1)} %copy-done.1), custom_call_target="tpu_custom_call" | custom-call | bytes 884736 | tf_op jit(solution)/shard_map/pallas_call | solution.py:361
  15.7 0.0 collective-permute-done.3
  15.7 0.7 add.11
  16.4 2.7 %collective-permute-done.2.m_ref.mate = bf16[8,256,128]{2,1,0:T(8,128)(2,1)S(1)} collective-permute-done((bf16[8,256,128]{2,1,0:T(8,128)(2,1)}, bf16[8,256,128]{2,1,0:T(8,128)(2,1)S(1)}, u32[]{:S(2)}, u32[]{:S(2)}) %collective-permute-start.2) | collective-permute-done | bytes 524320 | tf_op jit(solution)/shard_map/ppermute | solution.py:444
  19.1 4.7 %collective-permute-done.5.p_ref = bf16[8,256,128]{2,1,0:T(8,128)(2,1)S(1)} collective-permute-done((bf16[8,256,128]{2,1,0:T(8,128)(2,1)}, bf16[8,256,128]{2,1,0:T(8,128)(2,1)S(1)}, u32[]{:S(2)}, u32[]{:S(2)}) %collective-permute-start.5) | collective-permute-done | bytes 524320 | tf_op jit(solution)/shard_map/ppermute | solution.py:447
  23.8 0.1 collective-permute-start.6
  23.8 0.4 collective-permute-start.4
  24.2 1.0 %collective-permute-start.9 = (f32[8,128]{1,0:T(8,128)S(1)}, f32[8,128]{1,0:T(8,128)S(1)}, u32[]{:S(2)}, u32[]{:S(2)}) collective-permute-start(f32[8,128]{1,0:T(8,128)S(1)} %get-tuple-element.64), channel_id=1, source_target_pairs={{0,6},{2,4},{4,10},{6,8},{8,14},{10,12},{12,2},{14,0},{1,7},{3,5},... | collective-permute-start | bytes 12296 | tf_op jit(solution)/shard_map/ppermute | solution.py:450
  25.2 0.0 collective-permute-done.8.e_ref.eo_ref
  25.2 1.6 %collective-permute-start.7 = (f32[8,128]{1,0:T(8,128)S(1)}, f32[8,128]{1,0:T(8,128)S(1)}, u32[]{:S(2)}, u32[]{:S(2)}) collective-permute-start(f32[8,128]{1,0:T(8,128)S(1)} %get-tuple-element.63.t_ref.to_ref), channel_id=1, source_target_pairs={{0,4},{2,6},{4,8},{6,10},{8,12},{10,14},{12,0},{14,2},{1,5},{3,7},... | collective-permute-start | bytes 12296 | tf_op jit(solution)/shard_map/ppermute | solution.py:447
  26.7 2.5 %shard_map.112.in_ref = f32[8,256,256]{2,1,0:T(8,128)S(1)} custom-call(s32[3]{0:T(128)S(1)} %copy-done.3, bf16[8,256,128]{2,1,0:T(8,128)(2,1)S(1)} %copy-done, bf16[1,256,128]{2,1,0:T(8,128)(2,1)S(1)} %collective-permute-done.8.e_ref.eo_ref, f32[8,128]{1,0:T(8,128)S(1)} %get-tuple-element.63.t_ref.to_ref, f32[1,128]{1,0:T(1,128)S(1)} %bitcast.36, ...), custom_call_target="tpu_custom_call" | custom-call | flops 1207959552 | bytes 1184768 | tf_op jit(solution)/shard_map/pallas_call | solution.py:361
  29.3 0.0 collective-permute-done.p_ref
  29.3 1.6 %collective-permute-start.1 = (bf16[4,256,128]{2,1,0:T(8,128)(2,1)S(1)}, bf16[4,256,128]{2,1,0:T(8,128)(2,1)S(1)}, u32[]{:S(2)}, u32[]{:S(2)}) collective-permute-start(bf16[4,256,128]{2,1,0:T(8,128)(2,1)S(1)} %get-tuple-element.61), channel_id=1, source_target_pairs={{0,6},{2,4},{4,10},{6,8},{8,14},{10,12},{12,2},{14,0},{1,7},{3,5},... | collective-permute-start | bytes 786440 | tf_op jit(solution)/shard_map/ppermute | solution.py:450
  30.9 0.0 collective-permute-done.4.tm_ref
  30.9 0.1 collective-permute-start.10
  31.0 0.0 collective-permute-done.7.tp_ref
  31.0 0.0 collective-permute-done.9.tq_ref
  31.0 0.0 collective-permute-done.6.e_ref.em_ref
  31.0 0.0 copy-start.10
  31.0 4.7 %shard_map.113 = (f32[8,256,256]{2,1,0:T(8,128)S(1)}, f32[8,128]{1,0:T(8,128)S(1)}) custom-call(s32[3]{0:T(128)S(1)} %copy-done.3, bf16[8,256,128]{2,1,0:T(8,128)(2,1)S(1)} %collective-permute-done.2.m_ref.mate, f32[8,128]{1,0:T(8,128)S(1)} %collective-permute-done.4.tm_ref, bf16[8,256,128]{2,1,0:T(8,128)(2,1)S(1)} %collective-permute-done.5.p_ref, ...), custom_call_target="tpu_custom_call" | custom-call | flops 2415919104 | bytes 5063680 | tf_op jit(solution)/shard_map/pallas_call | solution.py:361
  35.7 0.0 collective-permute-done.10.ep_ref
  35.8 1.5 %shard_map.114 = (bf16[3,256,128]{2,1,0:T(8,128)(2,1)S(1)}, bf16[3,256,128]{2,1,0:T(8,128)(2,1)S(1)}, bf16[2,2,256,128]{3,2,1,0:T(8,128)(2,1)S(1)}, f32[2,8,128]{2,1,0:T(8,128)S(1)}) custom-call(s32[3]{0:T(128)S(1)} %copy-done.3, bf16[4,256,128]{2,1,0:T(8,128)(2,1)S(1)} %collective-permute-done.p_ref, ...), custom_call_target="tpu_custom_call" | custom-call | flops 452984832 | bytes 4264960 | tf_op jit(solution)/shard_map/pallas_call | solution.py:361
  37.2 2.6 %collective-permute-done.1.q_ref = bf16[4,256,128]{2,1,0:T(8,128)(2,1)S(1)} collective-permute-done((bf16[4,256,128]{2,1,0:T(8,128)(2,1)S(1)}, bf16[4,256,128]{2,1,0:T(8,128)(2,1)S(1)}, u32[]{:S(2)}, u32[]{:S(2)}) %collective-permute-start.1) | collective-permute-done | bytes 262176 | tf_op jit(solution)/shard_map/ppermute | solution.py:450
  39.9 2.0 %shard_map.115 = (bf16[4,256,128]{2,1,0:T(8,128)(2,1)S(1)}, bf16[5,256,128]{2,1,0:T(8,128)(2,1)S(1)}, bf16[4,256,128]{2,1,0:T(8,128)(2,1)S(1)}, f32[2,8,128]{2,1,0:T(8,128)S(1)}) custom-call(s32[3]{0:T(128)S(1)} %copy-done.3, bf16[4,256,128]{2,1,0:T(8,128)(2,1)S(1)} %collective-permute-done.p_ref, bf16[4,256,128]{2,1,0:T(8,128)(2,1)S(1)} %collective-permute-done.1.q_ref, ...), custom_call_target="tpu_custom_call" | custom-call | flops 754974720 | bytes 4469760 | tf_op jit(solution)/shard_map/pallas_call | solution.py:361
  41.8 0.1 collective-permute-start.16
  41.9 0.1 collective-permute-start.13
  42.0 1.8 %collective-permute-start.11 = (bf16[4,256,128]{2,1,0:T(8,128)(2,1)S(1)}, bf16[4,256,128]{2,1,0:T(8,128)(2,1)S(1)}, u32[]{:S(2)}, u32[]{:S(2)}) collective-permute-start(bf16[4,256,128]{2,1,0:T(8,128)(2,1)S(1)} %get-tuple-element.43.a1), channel_id=1, source_target_pairs={{0,4},{2,6},{4,8},{6,10},{8,12},{10,14},{12,0},{14,2},{1,5},{3,7},... | collective-permute-start | bytes 786440 | tf_op jit(solution)/shard_map/ppermute | solution.py:447
  43.8 0.8 %shard_map.116 = (bf16[1152,256]{1,0:T(8,128)(2,1)S(1)}, bf16[1152,256]{1,0:T(8,128)(2,1)S(1)}, bf16[1152,256]{1,0:T(8,128)(2,1)S(1)}, bf16[1152,128]{1,0:T(8,128)(2,1)S(1)}) custom-call(s32[3]{0:T(128)S(1)} %copy-done.3, bf16[3,3,3,128,128]{4,3,2,1,0:T(8,128)(2,1)S(1)} %copy-done.2), custom_call_target="tpu_custom_call" | custom-call | bytes 884736 | tf_op jit(solution)/shard_map/pallas_call | solution.py:361
  44.7 0.1 collective-permute-start.18
  44.8 0.4 collective-permute-start.14
  45.1 0.0 collective-permute-done.16
  45.1 2.9 %collective-permute-start.19 = (bf16[4,256,128]{2,1,0:T(8,128)(2,1)S(1)}, bf16[4,256,128]{2,1,0:T(8,128)(2,1)S(1)}, u32[]{:S(2)}, u32[]{:S(2)}) collective-permute-start(bf16[4,256,128]{2,1,0:T(8,128)(2,1)S(1)} %get-tuple-element.47.a2), channel_id=1, source_target_pairs={{0,4},{2,6},{4,8},{6,10},{8,12},{10,14},{12,0},{14,2},{1,5},{3,7},... | collective-permute-start | bytes 786440 | tf_op jit(solution)/shard_map/ppermute | solution.py:447
  48.0 3.6 %collective-permute-done.13.b1 = bf16[3,256,128]{2,1,0:T(8,128)(2,1)S(1)} collective-permute-done((bf16[3,256,128]{2,1,0:T(8,128)(2,1)S(1)}, bf16[3,256,128]{2,1,0:T(8,128)(2,1)S(1)}, u32[]{:S(2)}, u32[]{:S(2)}) %collective-permute-start.13) | collective-permute-done | bytes 196640 | tf_op jit(solution)/shard_map/ppermute | solution.py:447
  51.5 0.0 collective-permute-start.17
  51.6 5.6 %collective-permute-done.11.p1 = bf16[4,256,128]{2,1,0:T(8,128)(2,1)S(1)} collective-permute-done((bf16[4,256,128]{2,1,0:T(8,128)(2,1)S(1)}, bf16[4,256,128]{2,1,0:T(8,128)(2,1)S(1)}, u32[]{:S(2)}, u32[]{:S(2)}) %collective-permute-start.11) | collective-permute-done | bytes 262176 | tf_op jit(solution)/shard_map/ppermute | solution.py:447
  57.2 0.0 collective-permute-start.15
  57.2 0.0 collective-permute-done.18.e_ref
  57.2 0.6 collective-permute-start.12
  57.8 5.0 %shard_map.117.in_ref = f32[9,256,256]{2,1,0:T(8,128)S(1)} custom-call(s32[3]{0:T(128)S(1)} %copy-done.3, bf16[4,256,128]{2,1,0:T(8,128)(2,1)S(1)} %get-tuple-element.43.a1, bf16[4,256,128]{2,1,0:T(8,128)(2,1)S(1)} %get-tuple-element.47.a2, bf16[3,256,128]{2,1,0:T(8,128)(2,1)S(1)} %get-tuple-element.44.b1, bf16[5,256,128]{2,1,0:T(8,128)(2,1)S(1)} %get-tuple-element.45.b2, ...), custom_call_target="tpu_custom_call" | custom-call | flops 2717908992 | bytes 2499584 | tf_op jit(solution)/shard_map/pallas_call | solution.py:361
  62.8 6.7 %collective-permute-done.17.tp_ref = f32[2,8,128]{2,1,0:T(8,128)S(1)} collective-permute-done((f32[2,8,128]{2,1,0:T(8,128)S(1)}, f32[2,8,128]{2,1,0:T(8,128)S(1)}, u32[]{:S(2)}, u32[]{:S(2)}) %collective-permute-start.17) | collective-permute-done | bytes 8224 | tf_op jit(solution)/shard_map/ppermute | solution.py:447
  69.5 0.0 collective-permute-done.15.eb_ref
  69.5 0.0 collective-permute-done.14.b2
  69.5 4.1 %shard_map.118 = (f32[9,256,128]{2,1,0:T(8,128)S(1)}, bf16[4,128,128]{2,1,0:T(8,128)(2,1)S(1)}, f32[8,128]{1,0:T(8,128)S(1)}) custom-call(s32[3]{0:T(128)S(1)} %copy-done.3, bf16[3,256,128]{2,1,0:T(8,128)(2,1)S(1)} %collective-permute-done.13.b1, bf16[5,256,128]{2,1,0:T(8,128)(2,1)S(1)} %collective-permute-done.14.b2, ...), custom_call_target="tpu_custom_call" | custom-call | flops 1358954496 | bytes 5949952 | tf_op jit(solution)/shard_map/pallas_call | solution.py:361
  73.6 0.0 collective-permute-done.12.ep_ref
  73.6 1.8 %shard_map.119 = (bf16[4,256,128]{2,1,0:T(8,128)(2,1)S(1)}, bf16[1,128,128]{2,1,0:T(8,128)(2,1)S(1)}, bf16[1,128,128]{2,1,0:T(8,128)(2,1)S(1)}) custom-call(s32[3]{0:T(128)S(1)} %copy-done.3, bf16[4,256,128]{2,1,0:T(8,128)(2,1)S(1)} %collective-permute-done.11.p1, bf16[1,2,256,128]{3,2,1,0:T(8,128)(2,1)S(1)} %collective-permute-done.12.ep_ref, ...), custom_call_target="tpu_custom_call" | custom-call | flops 603979776 | bytes 4067840 | tf_op jit(solution)/shard_map/pallas_call | solution.py:361
  75.4 0.0 collective-permute-done.19.p2
  75.4 2.4 %shard_map.120 = (bf16[3,128,128]{2,1,0:T(8,128)(2,1)S(1)}, bf16[3,128,128]{2,1,0:T(8,128)(2,1)S(1)}) custom-call(s32[3]{0:T(128)S(1)} %copy-done.3, bf16[4,256,128]{2,1,0:T(8,128)(2,1)S(1)} %collective-permute-done.11.p1, bf16[4,256,128]{2,1,0:T(8,128)(2,1)S(1)} %collective-permute-done.19.p2, f32[8,128]{1,0:T(8,128)S(1)} %get-tuple-element.52.n_ref, ...), custom_call_target="tpu_custom_call" | custom-call | flops 754974720 | bytes 4264448 | tf_op jit(solution)/shard_map/pallas_call | solution.py:361
  77.8 0.6 collective-permute-start.21
  78.4 1.5 %collective-permute-start.20 = (bf16[1,128,128]{2,1,0:T(8,128)(2,1)S(1)}, bf16[1,128,128]{2,1,0:T(8,128)(2,1)S(1)}, u32[]{:S(2)}, u32[]{:S(2)}) collective-permute-start(bf16[1,128,128]{2,1,0:T(8,128)(2,1)S(1)} %get-tuple-element.59), channel_id=1, source_target_pairs={{0,2},{2,0},{4,6},{6,4},{8,10},{10,8},{12,14},{14,12},{1,3},{3,1},... | collective-permute-start | bytes 98312 | tf_op jit(solution)/shard_map/ppermute | solution.py:444
  79.9 3.0 %collective-permute-done.20.got1 = bf16[1,128,128]{2,1,0:T(8,128)(2,1)S(1)} collective-permute-done((bf16[1,128,128]{2,1,0:T(8,128)(2,1)S(1)}, bf16[1,128,128]{2,1,0:T(8,128)(2,1)S(1)}, u32[]{:S(2)}, u32[]{:S(2)}) %collective-permute-start.20) | collective-permute-done | bytes 32800 | tf_op jit(solution)/shard_map/ppermute | solution.py:444
  82.9 0.0 collective-permute-done.21.got2
  82.9 1.3 %shard_map.121 = bf16[2,4,128,128]{3,2,1,0:T(8,128)(2,1)} custom-call(s32[3]{0:T(128)S(1)} %copy-done.3, bf16[1,128,128]{2,1,0:T(8,128)(2,1)S(1)} %get-tuple-element.56.kept1, bf16[3,128,128]{2,1,0:T(8,128)(2,1)S(1)} %get-tuple-element.58.kept2, bf16[1,128,128]{2,1,0:T(8,128)(2,1)S(1)} %collective-permute-done.20.got1, ...), custom_call_target="tpu_custom_call" | custom-call | bytes 262144 | tf_op jit(solution)/shard_map/pallas_call | solution.py:361
  (32 shorter events, 0.1 us)
Async XLA Ops:
  0.0 14.6 %copy-start.1 = (bf16[3,3,3,128,128]{4,3,2,1,0:T(8,128)(2,1)S(1)}, bf16[3,3,3,128,128]{4,3,2,1,0:T(8,128)(2,1)}, u32[]{:S(2)}) copy-start(bf16[3,3,3,128,128]{4,3,2,1,0:T(8,128)(2,1)} %refs_0_.2) | copy-start | bytes 2654212
  0.7 13.9 %copy-start.3 = (s32[3]{0:T(128)S(1)}, s32[3]{0:T(128)}, u32[]{:S(2)}) copy-start(s32[3]{0:T(128)} %pad_add_fusion.flags) | copy-start | bytes 40
  3.8 22.9 %copy-start = (bf16[8,256,128]{2,1,0:T(8,128)(2,1)S(1)}, bf16[8,256,128]{2,1,0:T(8,128)(2,1)}, u32[]{:S(2)}) copy-start(bf16[8,256,128]{2,1,0:T(8,128)(2,1)} %get-tuple-element.34.own_ref.x_ref.o_ref.own) | copy-start | bytes 1572868
  3.8 22.9 %copy-start.7 = (f32[128]{0:T(128)S(1)}, f32[128]{0:T(128)}, u32[]{:S(2)}) copy-start(f32[128]{0:T(128)} %param.12) | copy-start | bytes 1540
  3.9 22.9 %copy-start.8 = (f32[128]{0:T(128)S(1)}, f32[128]{0:T(128)}, u32[]{:S(2)}) copy-start(f32[128]{0:T(128)} %param.13) | copy-start | bytes 1540
  3.9 15.2 %collective-permute-start.2 = (bf16[8,256,128]{2,1,0:T(8,128)(2,1)}, bf16[8,256,128]{2,1,0:T(8,128)(2,1)S(1)}, u32[]{:S(2)}, u32[]{:S(2)}) collective-permute-start(bf16[8,256,128]{2,1,0:T(8,128)(2,1)} %get-tuple-element.33.other_ref), channel_id=1, source_target_pairs={{0,2},{2,0},{4,6},{6,4},{8,10},{10,8},{12,14},{14,12},{1,3},{3,1},... | collective-permute-start | bytes 1572872 | tf_op jit(solution)/shard_map/ppermute | solution.py:444
  6.9 16.8 %collective-permute-start.5 = (bf16[8,256,128]{2,1,0:T(8,128)(2,1)}, bf16[8,256,128]{2,1,0:T(8,128)(2,1)S(1)}, u32[]{:S(2)}, u32[]{:S(2)}) collective-permute-start(bf16[8,256,128]{2,1,0:T(8,128)(2,1)} %get-tuple-element.34.own_ref.x_ref.o_ref.own), channel_id=1, source_target_pairs={{0,4},{2,6},{4,8},{6,10},{8,12},{10,14},{12,0},{14,2},{1,5},{3,7},... | collective-permute-start | bytes 1572872 | tf_op jit(solution)/shard_map/ppermute | solution.py:447
  10.6 5.1 %collective-permute-start.3 = (f32[2,8,128]{2,1,0:T(8,128)}, f32[2,8,128]{2,1,0:T(8,128)S(1)}, u32[]{:S(2)}, u32[]{:S(2)}) collective-permute-start(f32[2,8,128]{2,1,0:T(8,128)} %shard_map.110), channel_id=1, source_target_pairs={{0,1},{1,0},{2,3},{3,2},{4,5},{5,4},{6,7},{7,6},{8,9},{9,8},{10,11... | collective-permute-start | bytes 24584 | tf_op jit(solution)/shard_map/ppermute | solution.py:453
  11.4 13.7 %collective-permute-start.8 = (bf16[1,256,128]{2,1,0:T(8,128)(2,1)S(1)}, bf16[1,256,128]{2,1,0:T(8,128)(2,1)S(1)}, u32[]{:S(2)}, u32[]{:S(2)}) collective-permute-start(bf16[1,256,128]{2,1,0:T(8,128)(2,1)S(1)} %slice.36), channel_id=1, source_target_pairs={{0,1},{1,0},{2,3},{3,2},{4,5},{5,4},{6,7},{7,6},{8,9},{9,8},{10,11... | collective-permute-start | bytes 196616 | tf_op jit(solution)/shard_map/ppermute | solution.py:453
  13.0 16.3 %collective-permute-start = (bf16[4,256,128]{2,1,0:T(8,128)(2,1)S(1)}, bf16[4,256,128]{2,1,0:T(8,128)(2,1)S(1)}, u32[]{:S(2)}, u32[]{:S(2)}) collective-permute-start(bf16[4,256,128]{2,1,0:T(8,128)(2,1)S(1)} %get-tuple-element.62), channel_id=1, source_target_pairs={{0,6},{2,4},{4,10},{6,8},{8,14},{10,12},{12,2},{14,0},{1,7},{3,5},... | collective-permute-start | bytes 786440 | tf_op jit(solution)/shard_map/ppermute | solution.py:450
  23.8 7.2 %collective-permute-start.6 = (bf16[2,256,128]{2,1,0:T(8,128)(2,1)S(1)}, bf16[2,256,128]{2,1,0:T(8,128)(2,1)S(1)}, u32[]{:S(2)}, u32[]{:S(2)}) collective-permute-start(bf16[2,256,128]{2,1,0:T(8,128)(2,1)S(1)} %pad_maximum_fusion), channel_id=1, source_target_pairs={{0,1},{1,0},{2,3},{3,2},{4,5},{5,4},{6,7},{7,6},{8,9},{9,8},{10,11... | collective-permute-start | bytes 393224 | tf_op jit(solution)/shard_map/ppermute | solution.py:453
  23.8 7.0 %collective-permute-start.4 = (f32[8,128]{1,0:T(8,128)S(1)}, f32[8,128]{1,0:T(8,128)S(1)}, u32[]{:S(2)}, u32[]{:S(2)}) collective-permute-start(f32[8,128]{1,0:T(8,128)S(1)} %get-tuple-element.64), channel_id=1, source_target_pairs={{0,2},{2,0},{4,6},{6,4},{8,10},{10,8},{12,14},{14,12},{1,3},{3,1},... | collective-permute-start | bytes 12296 | tf_op jit(solution)/shard_map/ppermute | solution.py:444
  24.2 6.8 %collective-permute-start.9 = (f32[8,128]{1,0:T(8,128)S(1)}, f32[8,128]{1,0:T(8,128)S(1)}, u32[]{:S(2)}, u32[]{:S(2)}) collective-permute-start(f32[8,128]{1,0:T(8,128)S(1)} %get-tuple-element.64), channel_id=1, source_target_pairs={{0,6},{2,4},{4,10},{6,8},{8,14},{10,12},{12,2},{14,0},{1,7},{3,5},... | collective-permute-start | bytes 12296 | tf_op jit(solution)/shard_map/ppermute | solution.py:450
  25.2 5.8 %collective-permute-start.7 = (f32[8,128]{1,0:T(8,128)S(1)}, f32[8,128]{1,0:T(8,128)S(1)}, u32[]{:S(2)}, u32[]{:S(2)}) collective-permute-start(f32[8,128]{1,0:T(8,128)S(1)} %get-tuple-element.63.t_ref.to_ref), channel_id=1, source_target_pairs={{0,4},{2,6},{4,8},{6,10},{8,12},{10,14},{12,0},{14,2},{1,5},{3,7},... | collective-permute-start | bytes 12296 | tf_op jit(solution)/shard_map/ppermute | solution.py:447
  29.3 10.5 %collective-permute-start.1 = (bf16[4,256,128]{2,1,0:T(8,128)(2,1)S(1)}, bf16[4,256,128]{2,1,0:T(8,128)(2,1)S(1)}, u32[]{:S(2)}, u32[]{:S(2)}) collective-permute-start(bf16[4,256,128]{2,1,0:T(8,128)(2,1)S(1)} %get-tuple-element.61), channel_id=1, source_target_pairs={{0,6},{2,4},{4,10},{6,8},{8,14},{10,12},{12,2},{14,0},{1,7},{3,5},... | collective-permute-start | bytes 786440 | tf_op jit(solution)/shard_map/ppermute | solution.py:450
  30.9 4.9 %collective-permute-start.10 = (bf16[1,256,128]{2,1,0:T(8,128)(2,1)S(1)}, bf16[1,256,128]{2,1,0:T(8,128)(2,1)S(1)}, u32[]{:S(2)}, u32[]{:S(2)}) collective-permute-start(bf16[1,256,128]{2,1,0:T(8,128)(2,1)S(1)} %slice.44), channel_id=1, source_target_pairs={{0,1},{1,0},{2,3},{3,2},{4,5},{5,4},{6,7},{7,6},{8,9},{9,8},{10,11... | collective-permute-start | bytes 196616 | tf_op jit(solution)/shard_map/ppermute | solution.py:453
  31.0 4.8 %copy-start.10 = (f32[128]{0:T(128)S(1)}, f32[128]{0:T(128)}, u32[]{:S(2)}) copy-start(f32[128]{0:T(128)} %param.15) | copy-start | bytes 1540
  39.8 3.9 %copy-start.9 = (bf16[3,3,128,128]{3,2,1,0:T(8,128)(2,1)S(1)}, bf16[3,3,128,128]{3,2,1,0:T(8,128)(2,1)}, u32[]{:S(2)}) copy-start(bf16[3,3,128,128]{3,2,1,0:T(8,128)(2,1)} %param.20) | copy-start | bytes 884740
  39.9 4.0 %copy-start.2 = (bf16[3,3,3,128,128]{4,3,2,1,0:T(8,128)(2,1)S(1)}, bf16[3,3,3,128,128]{4,3,2,1,0:T(8,128)(2,1)}, u32[]{:S(2)}) copy-start(bf16[3,3,3,128,128]{4,3,2,1,0:T(8,128)(2,1)} %refs_0_.3) | copy-start | bytes 2654212
  39.9 17.9 %copy-start.5 = (f32[128]{0:T(128)S(1)}, f32[128]{0:T(128)}, u32[]{:S(2)}) copy-start(f32[128]{0:T(128)} %param.16) | copy-start | bytes 1540
  39.9 17.9 %copy-start.6 = (f32[128]{0:T(128)S(1)}, f32[128]{0:T(128)}, u32[]{:S(2)}) copy-start(f32[128]{0:T(128)} %param.17) | copy-start | bytes 1540
  41.8 3.3 %collective-permute-start.16 = (f32[2,8,128]{2,1,0:T(8,128)S(1)}, f32[2,8,128]{2,1,0:T(8,128)S(1)}, u32[]{:S(2)}, u32[]{:S(2)}) collective-permute-start(f32[2,8,128]{2,1,0:T(8,128)S(1)} %get-tuple-element.46), channel_id=1, source_target_pairs={{0,1},{1,0},{2,3},{3,2},{4,5},{5,4},{6,7},{7,6},{8,9},{9,8},{10,11... | collective-permute-start | bytes 24584 | tf_op jit(solution)/shard_map/ppermute | solution.py:453
  41.9 9.6 %collective-permute-start.13 = (bf16[3,256,128]{2,1,0:T(8,128)(2,1)S(1)}, bf16[3,256,128]{2,1,0:T(8,128)(2,1)S(1)}, u32[]{:S(2)}, u32[]{:S(2)}) collective-permute-start(bf16[3,256,128]{2,1,0:T(8,128)(2,1)S(1)} %get-tuple-element.44.b1), channel_id=1, source_target_pairs={{0,4},{2,6},{4,8},{6,10},{8,12},{10,14},{12,0},{14,2},{1,5},{3,7},... | collective-permute-start | bytes 589832 | tf_op jit(solution)/shard_map/ppermute | solution.py:447
  42.0 15.2 %collective-permute-start.11 = (bf16[4,256,128]{2,1,0:T(8,128)(2,1)S(1)}, bf16[4,256,128]{2,1,0:T(8,128)(2,1)S(1)}, u32[]{:S(2)}, u32[]{:S(2)}) collective-permute-start(bf16[4,256,128]{2,1,0:T(8,128)(2,1)S(1)} %get-tuple-element.43.a1), channel_id=1, source_target_pairs={{0,4},{2,6},{4,8},{6,10},{8,12},{10,14},{12,0},{14,2},{1,5},{3,7},... | collective-permute-start | bytes 786440 | tf_op jit(solution)/shard_map/ppermute | solution.py:447
  44.7 12.5 %collective-permute-start.18 = (bf16[2,2,256,128]{3,2,1,0:T(8,128)(2,1)S(1)}, bf16[2,2,256,128]{3,2,1,0:T(8,128)(2,1)S(1)}, u32[]{:S(2)}, u32[]{:S(2)}) collective-permute-start(bf16[2,2,256,128]{3,2,1,0:T(8,128)(2,1)S(1)} %get-tuple-element.48), channel_id=1, source_target_pairs={{0,1},{1,0},{2,3},{3,2},{4,5},{5,4},{6,7},{7,6},{8,9},{9,8},{10,11... | collective-permute-start | bytes 786440 | tf_op jit(solution)/shard_map/ppermute | solution.py:453
  44.8 24.7 %collective-permute-start.14 = (bf16[5,256,128]{2,1,0:T(8,128)(2,1)S(1)}, bf16[5,256,128]{2,1,0:T(8,128)(2,1)S(1)}, u32[]{:S(2)}, u32[]{:S(2)}) collective-permute-start(bf16[5,256,128]{2,1,0:T(8,128)(2,1)S(1)} %get-tuple-element.45.b2), channel_id=1, source_target_pairs={{0,4},{2,6},{4,8},{6,10},{8,12},{10,14},{12,0},{14,2},{1,5},{3,7},... | collective-permute-start | bytes 983048 | tf_op jit(solution)/shard_map/ppermute | solution.py:447
  45.1 30.3 %collective-permute-start.19 = (bf16[4,256,128]{2,1,0:T(8,128)(2,1)S(1)}, bf16[4,256,128]{2,1,0:T(8,128)(2,1)S(1)}, u32[]{:S(2)}, u32[]{:S(2)}) collective-permute-start(bf16[4,256,128]{2,1,0:T(8,128)(2,1)S(1)} %get-tuple-element.47.a2), channel_id=1, source_target_pairs={{0,4},{2,6},{4,8},{6,10},{8,12},{10,14},{12,0},{14,2},{1,5},{3,7},... | collective-permute-start | bytes 786440 | tf_op jit(solution)/shard_map/ppermute | solution.py:447
  51.5 17.9 %collective-permute-start.17 = (f32[2,8,128]{2,1,0:T(8,128)S(1)}, f32[2,8,128]{2,1,0:T(8,128)S(1)}, u32[]{:S(2)}, u32[]{:S(2)}) collective-permute-start(f32[2,8,128]{2,1,0:T(8,128)S(1)} %add.12.t_ref), channel_id=1, source_target_pairs={{0,4},{2,6},{4,8},{6,10},{8,12},{10,14},{12,0},{14,2},{1,5},{3,7},... | collective-permute-start | bytes 24584 | tf_op jit(solution)/shard_map/ppermute | solution.py:447
  57.2 12.3 %collective-permute-start.15 = (bf16[1,2,256,128]{3,2,1,0:T(8,128)(2,1)S(1)}, bf16[1,2,256,128]{3,2,1,0:T(8,128)(2,1)S(1)}, u32[]{:S(2)}, u32[]{:S(2)}) collective-permute-start(bf16[1,2,256,128]{3,2,1,0:T(8,128)(2,1)S(1)} %slice_bitcast_fusion), channel_id=1, source_target_pairs={{0,1},{1,0},{2,3},{3,2},{4,5},{5,4},{6,7},{7,6},{8,9},{9,8},{10,11... | collective-permute-start | bytes 393224 | tf_op jit(solution)/shard_map/ppermute | solution.py:453
  57.2 16.4 %collective-permute-start.12 = (bf16[1,2,256,128]{3,2,1,0:T(8,128)(2,1)S(1)}, bf16[1,2,256,128]{3,2,1,0:T(8,128)(2,1)S(1)}, u32[]{:S(2)}, u32[]{:S(2)}) collective-permute-start(bf16[1,2,256,128]{3,2,1,0:T(8,128)(2,1)S(1)} %slice_bitcast_fusion.1), channel_id=1, source_target_pairs={{0,1},{1,0},{2,3},{3,2},{4,5},{5,4},{6,7},{7,6},{8,9},{9,8},{10,11... | collective-permute-start | bytes 393224 | tf_op jit(solution)/shard_map/ppermute | solution.py:453
  57.8 11.7 %copy-start.11 = (f32[128]{0:T(128)S(1)}, f32[128]{0:T(128)}, u32[]{:S(2)}) copy-start(f32[128]{0:T(128)} %param.19) | copy-start | bytes 1540
  57.8 11.7 %copy-start.4 = (f32[128]{0:T(128)S(1)}, f32[128]{0:T(128)}, u32[]{:S(2)}) copy-start(f32[128]{0:T(128)} %param.21) | copy-start | bytes 1540
  77.8 5.1 %collective-permute-start.21 = (bf16[3,128,128]{2,1,0:T(8,128)(2,1)S(1)}, bf16[3,128,128]{2,1,0:T(8,128)(2,1)S(1)}, u32[]{:S(2)}, u32[]{:S(2)}) collective-permute-start(bf16[3,128,128]{2,1,0:T(8,128)(2,1)S(1)} %get-tuple-element.60), channel_id=1, source_target_pairs={{0,2},{2,0},{4,6},{6,4},{8,10},{10,8},{12,14},{14,12},{1,3},{3,1},... | collective-permute-start | bytes 294920 | tf_op jit(solution)/shard_map/ppermute | solution.py:444
  78.4 4.5 %collective-permute-start.20 = (bf16[1,128,128]{2,1,0:T(8,128)(2,1)S(1)}, bf16[1,128,128]{2,1,0:T(8,128)(2,1)S(1)}, u32[]{:S(2)}, u32[]{:S(2)}) collective-permute-start(bf16[1,128,128]{2,1,0:T(8,128)(2,1)S(1)} %get-tuple-element.59), channel_id=1, source_target_pairs={{0,2},{2,0},{4,6},{6,4},{8,10},{10,8},{12,14},{14,12},{1,3},{3,1},... | collective-permute-start | bytes 98312 | tf_op jit(solution)/shard_map/ppermute | solution.py:444
